TPU v7x, 32 devices: a whole 2x2x4 slice. The times are simulated.
32 devices in a mesh: parts: 2 (over y), space: 8 (over z, x), dp: 2 (over core).
Axes of the slice: x: 2, y: 2, z: 4, core: 2. Of those that a mesh axis runs over, the one named last changes fastest.
Arguments:
- volume: bfloat16 [4, 128, 32, 128, 128], P(('parts', 'dp'), 'space'), parts along dimension 0, may hold values from -6 to 6
- cotangent: bfloat16 [4, 128, 32, 128, 128], P(('parts', 'dp'), 'space'), parts along dimension 0, may hold values from -6 to 6
- spectral_weight: bfloat16 [2, 32, 512, 32, 32], P(None, None, 'space')
- pointwise_weight: bfloat16 [32, 32], replicated, may hold values from -1 to 1
- gain_table: bfloat16 [4096, 32], replicated, may hold values from 0.099609375 to 1.8984375
- bias_index: int32 [4], P(('parts', 'dp')), parts along dimension 0, may hold values from 0 to 4095
Outputs:
- input_grad: bfloat16 [4, 128, 32, 128, 128], P(('parts', 'dp'), 'space'), parts along dimension 0
- spectral_grad: float32 [4, 32, 512, 32, 32], P('parts', None, 'space', None, 'dp'), parts along dimension 0
There are 2 independent parts, one for each index of `parts`. A program takes and returns all parts, laid end to end along the dimension named above; an argument that names none is the same for every part. Nothing has to cross between parts.
All inputs are finite; a program needn't handle non-finite values.
Results may differ from a plain program's by a relative error of at most 0.01.
Values may be sent and summed in bfloat16 or wider, within the bound.
No kernel may reach another device: no remote copies, remote signals or barrier semaphores. Data moves between devices by JAX's collectives and lax.ppermute only.
A program may use at most 256 MiB of HBM per device.

v0:
```python
import functools
import math

import jax
import jax.numpy as jnp
import numpy as np
from jax import lax
from jax.experimental import pallas as pl
from jax.experimental.pallas import tpu as pltpu
from jax.sharding import PartitionSpec as P

M = 16
NX = 128
NY = 128
NZ = 128


def trig_tables(length, modes_count, signed):
    positions = jnp.arange(length, dtype=jnp.int32)
    mode_base = jnp.arange(modes_count, dtype=jnp.int32)
    if signed:
        frequency = jnp.concatenate([mode_base, mode_base - modes_count])
    else:
        frequency = mode_base
    phase_index = jnp.mod(positions[:, None] * frequency[None, :], length)
    angles = phase_index.astype(jnp.float32) * (2.0 * math.pi / length)
    return (jnp.cos(angles).astype(jnp.bfloat16), jnp.sin(angles).astype(jnp.bfloat16))


def general_device(volume, cotangent, spectral_weight, pointwise_weight, gain_table, bias_index):
    cos_z, sin_z = trig_tables(NZ, M, False)
    cos_y, sin_y = trig_tables(NY, M, True)
    cos_x, sin_x = trig_tables(NX, M, True)
    table_z = jnp.concatenate([cos_z, -sin_z], axis=1)
    table_y = jnp.concatenate([cos_y, sin_y], axis=1)
    paired_y = jnp.stack([cos_y, sin_y], axis=1)
    table_x = jnp.concatenate([cos_x, sin_x], axis=1)
    paired_x = jnp.stack([cos_x, sin_x], axis=1)
    ortho_scale = 1.0 / math.sqrt(NX * NY * NZ)
    pair_count = spectral_weight.shape[2]
    global_pairs = lax.axis_index("space") * pair_count + jnp.arange(pair_count, dtype=jnp.int32)
    flat_scale = jnp.full((pair_count,), ortho_scale, dtype=jnp.float32)
    doubled_scale = jnp.where(global_pairs % M == 0, 1.0, 2.0).astype(jnp.float32) * ortho_scale

    def lateral_spectrum(values_in):
        along_z = jnp.einsum(
            "sxcyz,zk->sxcky", values_in, table_z, preferred_element_type=jnp.float32
        ).astype(jnp.bfloat16)
        products = jnp.einsum(
            "sxcky,yj->sxckj", along_z, table_y, preferred_element_type=jnp.float32
        )
        real_part = products[:, :, :, :M, : 2 * M] + products[:, :, :, M:, 2 * M :]
        imag_part = products[:, :, :, M:, : 2 * M] - products[:, :, :, :M, 2 * M :]
        stacked = jnp.swapaxes(jnp.stack([real_part, imag_part], axis=2), 4, 5).astype(jnp.bfloat16)
        return stacked.reshape(stacked.shape[0], stacked.shape[1], 2, stacked.shape[3], 2 * M * M)

    def axial_spectrum(received, pair_scale):
        products = jnp.einsum(
            "sxrcp,xj->srjpc", received, table_x, preferred_element_type=jnp.float32
        )
        real_part = products[:, 0, : 2 * M] + products[:, 1, 2 * M :]
        imag_part = products[:, 1, : 2 * M] - products[:, 0, 2 * M :]
        stacked = jnp.stack([real_part, imag_part], axis=1)
        return (stacked * pair_scale[None, None, None, :, None]).astype(jnp.bfloat16)

    volume_hat = axial_spectrum(
        lax.all_to_all(lateral_spectrum(volume), "space", split_axis=4, concat_axis=1, tiled=True),
        flat_scale,
    )
    cotangent_hat = axial_spectrum(
        lax.all_to_all(
            lateral_spectrum(cotangent), "space", split_axis=4, concat_axis=1, tiled=True
        ),
        doubled_scale,
    )
    grad_real = jnp.einsum(
        "sapc,sapo->apco", volume_hat[:, 0], cotangent_hat[:, 0], preferred_element_type=jnp.float32
    ) + jnp.einsum(
        "sapc,sapo->apco", volume_hat[:, 1], cotangent_hat[:, 1], preferred_element_type=jnp.float32
    )
    grad_imag = jnp.einsum(
        "sapc,sapo->apco", volume_hat[:, 0], cotangent_hat[:, 1], preferred_element_type=jnp.float32
    ) - jnp.einsum(
        "sapc,sapo->apco", volume_hat[:, 1], cotangent_hat[:, 0], preferred_element_type=jnp.float32
    )
    spectral_grad = lax.psum_scatter(
        jnp.stack([grad_real, grad_imag]).astype(jnp.bfloat16),
        "dp",
        scatter_dimension=4,
        tiled=True,
    ).astype(jnp.float32)
    weight_real = spectral_weight[0]
    weight_imag = spectral_weight[1]
    cot_real = cotangent_hat[:, 0]
    cot_imag = cotangent_hat[:, 1]
    back_real = jnp.einsum(
        "apco,sapo->sapc", weight_real, cot_real, preferred_element_type=jnp.float32
    ) + jnp.einsum("apco,sapo->sapc", weight_imag, cot_imag, preferred_element_type=jnp.float32)
    back_imag = jnp.einsum(
        "apco,sapo->sapc", weight_real, cot_imag, preferred_element_type=jnp.float32
    ) - jnp.einsum("apco,sapo->sapc", weight_imag, cot_real, preferred_element_type=jnp.float32)
    back_modes = jnp.stack([back_real, back_imag], axis=1).astype(jnp.bfloat16)
    products = jnp.einsum(
        "srapc,xta->srtxcp", back_modes, paired_x, preferred_element_type=jnp.float32
    )
    plane_real = products[:, 0, 0] - products[:, 1, 1]
    plane_imag = products[:, 0, 1] + products[:, 1, 0]
    back_planes = jnp.stack([plane_real, plane_imag], axis=2).astype(jnp.bfloat16)
    received = lax.all_to_all(back_planes, "space", split_axis=1, concat_axis=4, tiled=True)
    mode_grid = received.reshape(
        received.shape[0], received.shape[1], 2, received.shape[3], 2 * M, M
    )
    row_products = jnp.einsum(
        "nxrcbd,ytb->nxrtcyd", mode_grid, paired_y, preferred_element_type=jnp.float32
    )
    row_real = row_products[:, :, 0, 0] - row_products[:, :, 1, 1]
    row_imag = row_products[:, :, 0, 1] + row_products[:, :, 1, 0]
    row_values = jnp.concatenate([row_real, row_imag], axis=4).astype(jnp.bfloat16)
    spectral_part = (
        jnp.einsum("nxcyk,kz->nxcyz", row_values, table_z.T, preferred_element_type=jnp.float32)
        * ortho_scale
    )
    bias_rows = (
        bias_index[:, None] == jnp.arange(gain_table.shape[0], dtype=jnp.int32)[None, :]
    ).astype(jnp.bfloat16)
    gain_rows = jnp.dot(bias_rows, gain_table, preferred_element_type=jnp.float32)
    scaled = (cotangent * gain_rows[:, None, :, None, None]).astype(jnp.bfloat16)
    pointwise_part = jnp.einsum(
        "co,sxoyz->sxcyz", pointwise_weight, scaled, preferred_element_type=jnp.float32
    )
    return ((spectral_part + pointwise_part).astype(jnp.bfloat16), spectral_grad)


BF = jnp.bfloat16
F32 = jnp.float32
ORTHO = 1.0 / math.sqrt(NX * NY * NZ)


def host_tables(length, modes_count, signed):
    frequency = np.arange(modes_count)
    if signed:
        frequency = np.concatenate([frequency, frequency - modes_count])
    phase = np.mod(np.arange(length)[:, None] * frequency[None, :], length)
    angles = phase.astype(np.float32) * np.float32(2.0 * math.pi / length)
    cos = np.cos(angles).astype(jnp.bfloat16).astype(np.float32)
    sin = np.sin(angles).astype(jnp.bfloat16).astype(np.float32)
    return cos, sin


def fixed_operands():
    cz, sz = host_tables(NZ, M, False)
    cy, sy = host_tables(NY, M, True)
    cx, sx = host_tables(NX, M, True)
    z_ops = np.zeros((8, NZ, 2, 8, M), np.float32)
    for c in range(8):
        z_ops[c, :, 0, c] = cz
        z_ops[c, :, 1, c] = -sz
    z_ops = z_ops.reshape(8 * NZ, 16 * M)
    y_all = np.stack([np.concatenate([cy.T, sy.T], 1), np.concatenate([-sy.T, cy.T], 1)], 1)
    y_all = y_all.reshape(8, 4, 2, 2 * NY)
    x_all = np.stack([np.stack([cx.T, sx.T], 1), np.stack([-sx.T, cx.T], 1)], 0)
    x_all = x_all.reshape(2, M, 2, 2, 8, 16).transpose(2, 0, 1, 3, 4, 5)
    order = [[[s ^ (4 * j + k) for j in range(2)] for k in range(4)] for s in range(8)]
    y_ops = np.stack([y_all[order[s]] for s in range(8)]).reshape(8, 64, 2 * NY)
    x_ops = np.stack([x_all[..., [s ^ k for k in range(4)], :] for s in range(8)])
    x_ops = x_ops.reshape(8, 64, NX)
    shuffle = np.zeros((4, 8, M, 8, 2, 4, M), np.float32)
    for b in range(4):
        for c in range(8):
            for d in range(M):
                shuffle[b, c, d, c, :, b, d] = 1.0
    shuffle = shuffle.reshape(32 * M, 64 * M)
    ops = dict(z_fwd=z_ops, z_back=z_ops.T, y=y_ops, x=x_ops, spread=shuffle)
    return {k: jnp.asarray(np.ascontiguousarray(v).astype(jnp.bfloat16)) for k, v in ops.items()}


def dot(a, b):
    return jnp.dot(a, b, preferred_element_type=F32)


def params(mib):
    return pltpu.CompilerParams(vmem_limit_bytes=mib << 20)


def cost(us, mib=1):
    return pl.CostEstimate(
        flops=int(us * 6e6), bytes_accessed=mib << 10, transcendentals=0
    )


VMEM = pl.BlockSpec(memory_space=pltpu.VMEM)
SMEM = pl.BlockSpec(memory_space=pltpu.SMEM)
HBM = pl.BlockSpec(memory_space=pltpu.HBM)
UNREAD = pl.BlockSpec(memory_space=pl.ANY)


def in_vmem(x):
    return pltpu.with_memory_space_constraint(x, pltpu.VMEM)


def in_hbm(x):
    return pltpu.with_memory_space_constraint(x, pltpu.HBM)


GROUP = 4
SLOTS = 12


def lateral_kernel(me_ref, v_ref, z_hbm, y_hbm, _, *rest):
    outs, (s_ref, z_ref, y_ref, b_ref, sem, z_sem) = rest[:4], rest[4:]
    nx = v_ref.shape[0]

    def copy(x):
        slot = lax.rem(x, SLOTS)
        return pltpu.make_async_copy(v_ref.at[x], b_ref.at[slot], sem.at[slot])

    tables = [
        pltpu.make_async_copy(z_hbm, z_ref, z_sem.at[0]),
        pltpu.make_async_copy(y_hbm.at[me_ref[0]], y_ref, z_sem.at[1]),
    ]
    for x in range(GROUP):
        copy(x).start()
    for table in tables:
        table.start()
    for x in range(GROUP, SLOTS - GROUP):
        copy(x).start()
    for table in tables:
        table.wait()

    def one(i, carry):
        for k in range(GROUP):
            x = i * GROUP + k
            ahead = x + SLOTS - GROUP

            @pl.when(ahead < nx)
            def _():
                copy(ahead).start()

            copy(x).wait()
        rows = [
            jnp.concatenate(
                [b_ref[lax.rem(i * GROUP + k, SLOTS), co * 8 + c] for c in range(8)], axis=1
            )
            for k in range(GROUP)
            for co in range(4)
        ]
        along = dot(jnp.concatenate(rows, axis=0), z_ref[...]).astype(BF)
        for k in range(GROUP):
            for h in range(2):
                at = (k * 2 + h) * 256
                lo = along[at : at + 128]
                hi = along[at + 128 : at + 256]
                rhs = jnp.concatenate(
                    [
                        jnp.concatenate([lo[:, :128], hi[:, :128]], axis=1),
                        jnp.concatenate([lo[:, 128:], hi[:, 128:]], axis=1),
                    ],
                    axis=0,
                )
                out = dot(y_ref[...], rhs)
                for j in range(2):
                    s_ref[h * 2 + j, pl.ds(i * GROUP + k, 64, stride=16), :] = out[
                        :, j * 128 : j * 128 + 128
                    ]
        return carry

    lax.fori_loop(0, nx // GROUP, one, 0)
    for r in range(64):
        q, j, k = r // 16, (r // 8) % 2, r % 8
        for n in range(4):
            cut = s_ref[n, r * 16 : r * 16 + 16, :].astype(BF)
            outs[q][j, :, k * 512 + n * 128 : k * 512 + n * 128 + 128] = cut


def lateral(me, values, ops, first, name):
    nx = values.shape[0]
    return pl.pallas_call(
        lateral_kernel,
        in_specs=[SMEM, HBM, HBM, HBM, UNREAD],
        out_specs=[VMEM] * 4,
        out_shape=[jax.ShapeDtypeStruct((2, nx, 4096), BF)] * 4,
        scratch_shapes=[
            pltpu.VMEM((4, nx * 64, 128), F32),
            pltpu.VMEM((1024, 256), BF),
            pltpu.VMEM((64, 256), BF),
            pltpu.VMEM((SLOTS, 32, NY, NZ), BF),
            pltpu.SemaphoreType.DMA((SLOTS,)),
            pltpu.SemaphoreType.DMA((2,)),
        ],
        compiler_params=params(20),
        cost_estimate=cost(10),
        name=name,
    )(me, in_hbm(values), in_hbm(ops["z_fwd"]), in_hbm(ops["y"]), first)


def square_sum(table, refs, j, b):
    rhs = jnp.concatenate(
        [ref[j, :, pl.ds(b * 1024 + part * 512, 512)] for part in range(2) for ref in refs],
        axis=0,
    )
    return dot(table, rhs)


def partner_kernel(me_ref, r0, r1, r2, r3, x_hbm, _, o_ref, __, x_ref, sem):
    copy = pltpu.make_async_copy(x_hbm.at[me_ref[0]], x_ref, sem)
    copy.start()
    copy.wait()
    for b in range(4):
        o_ref[:, pl.ds(b * 512, 512)] = square_sum(x_ref[...], (r0, r1, r2, r3), 1, b).astype(BF)


def partner_modes(me, received, ops, passed, name):
    return pl.pallas_call(
        partner_kernel,
        in_specs=[SMEM] + [VMEM] * 4 + [HBM, UNREAD],
        out_specs=[VMEM, UNREAD],
        out_shape=[
            jax.ShapeDtypeStruct((64, 2048), BF),
            jax.ShapeDtypeStruct(passed.shape, passed.dtype),
        ],
        input_output_aliases={6: 1},
        scratch_shapes=[pltpu.VMEM((64, NX), BF), pltpu.SemaphoreType.DMA(())],
        compiler_params=params(16),
        cost_estimate=cost(1),
        name=name,
    )(me, *received, in_hbm(ops["x"]), passed)


def axial_modes(table, refs, other_ref, spread_ref, ready, doubled, store):
    lane = lax.broadcasted_iota(jnp.int32, (1, 512), 1)
    scale = jnp.where(lane % M == 0, ORTHO, (2.0 if doubled else 1.0) * ORTHO).astype(F32)
    cuts = [
        (
            (square_sum(table, refs, 0, b) + other_ref[:, pl.ds(b * 512, 512)].astype(F32)) * scale
        ).astype(BF)
        for b in range(4)
    ]
    both = jnp.concatenate(
        [
            jnp.concatenate(
                [cut[a2 * 32 : a2 * 32 + 32, co * 128 : co * 128 + 128] for cut in cuts], axis=1
            )
            for a2 in range(2)
            for co in range(4)
        ],
        axis=0,
    )
    low = lax.broadcasted_iota(jnp.int32, (128, 128), 1) < 64
    ready()
    for c in range(0, 8, 2):
        moved = dot(both, spread_ref[:, pl.ds(c * 128, 256)])
        for k in range(2):
            cut = moved[:, k * 128 : k * 128 + 128]
            store(c + k, jnp.where(low, cut[:128], cut[128:]))


def volume_modes_kernel(
    me_ref, r0, r1, r2, r3, other_ref, x_hbm, spread_hbm, *rest
):
    o_ref, x_ref, spread_ref, sem = rest[-4:]
    copies = [
        pltpu.make_async_copy(x_hbm.at[me_ref[0]], x_ref, sem.at[0]),
        pltpu.make_async_copy(spread_hbm, spread_ref, sem.at[1]),
    ]
    for copy in copies:
        copy.start()

    def store(c, value):
        for co in range(4):
            o_ref[co * 8 + c] = value[co * 32 : co * 32 + 32].astype(BF)

    copies[0].wait()
    axial_modes(
        x_ref[...], (r0, r1, r2, r3), other_ref, spread_ref, copies[1].wait, False, store
    )


MODE_SCRATCH = [
    pltpu.VMEM((64, NX), BF),
    pltpu.VMEM((512, 1024), BF),
    pltpu.SemaphoreType.DMA((2,)),
]


def volume_modes(me, received, other, ops, ahead):
    return pl.pallas_call(
        volume_modes_kernel,
        in_specs=[SMEM] + [VMEM] * 5 + [HBM] * 2 + [UNREAD] * len(ahead),
        out_specs=VMEM,
        out_shape=jax.ShapeDtypeStruct((32, 32, 128), BF),
        scratch_shapes=MODE_SCRATCH,
        compiler_params=params(16),
        cost_estimate=cost(1.5),
        name="volume_modes",
    )(me, *received, other, in_hbm(ops["x"]), in_hbm(ops["spread"]), *ahead)


def kron_operand(at, p_ref, gain_ref):
    lane = lax.broadcasted_iota(jnp.int32, (32, 128), 1)
    here = lane == lax.rem(at, 128)
    gain = jnp.sum(jnp.where(here, gain_ref[...].astype(F32), 0.0), axis=1, keepdims=True)
    wide = (
        lax.broadcasted_iota(jnp.int32, (32, 256), 0)
        == lax.broadcasted_iota(jnp.int32, (32, 256), 1) // 8
    )
    tall = (
        lax.broadcasted_iota(jnp.int32, (256, 32), 0) // 8
        == lax.broadcasted_iota(jnp.int32, (256, 32), 1)
    )
    gains = jnp.sum(jnp.where(wide, gain, 0.0), axis=0, keepdims=True)
    kron = dot(tall.astype(F32).astype(BF), p_ref[...]).astype(BF)
    kron = dot(kron, wide.astype(F32).astype(BF)) * gains
    same = lax.rem(lax.broadcasted_iota(jnp.int32, (256, 256), 0), 8) == lax.rem(
        lax.broadcasted_iota(jnp.int32, (256, 256), 1), 8
    )
    return jnp.where(same, kron, 0.0).astype(BF)


def pack_kernel(
    at_ref, w_hbm, p_ref, g_hbm, _, o_ref, k_ref, w_ref, gain_ref, sem, gain_sem
):
    block = pl.multiple_of(at_ref[0] // 128 * 128, 128)
    gains = pltpu.make_async_copy(g_hbm.at[:, pl.ds(block, 128)], gain_ref, gain_sem)
    gains.start()
    slots = w_ref.shape[0]

    def copy(i):
        slot = lax.rem(i, slots)
        return pltpu.make_async_copy(w_hbm.at[:, pl.ds(2 * i, 2)], w_ref.at[slot], sem.at[slot])

    for i in range(slots - 1):
        copy(i).start()

    gains.wait()
    k_ref[...] = kron_operand(at_ref[0], p_ref, gain_ref)

    def one(i, carry):
        @pl.when(i + slots - 1 < M)
        def _():
            copy(i + slots - 1).start()

        copy(i).wait()
        slot = lax.rem(i, slots)
        for part in range(2):
            o_ref[part, i] = jnp.concatenate(
                [w_ref[slot, part, 0], w_ref[slot, part, 1]], axis=-1
            )
        return carry

    lax.fori_loop(0, M, one, 0)


def pack_weight(bias_index, weight, pointwise_weight, gain_table, first):
    return pl.pallas_call(
        pack_kernel,
        in_specs=[SMEM, HBM, VMEM, HBM, UNREAD],
        out_specs=[VMEM, VMEM],
        out_shape=[
            pltpu.VMEM((2, M, 32, 32, 128), BF),
            jax.ShapeDtypeStruct((256, 256), BF),
        ],
        scratch_shapes=[
            pltpu.VMEM((9, 2, 2, 32, 32, 64), BF),
            pltpu.VMEM((32, 128), BF),
            pltpu.SemaphoreType.DMA((9,)),
            pltpu.SemaphoreType.DMA(()),
        ],
        compiler_params=params(16),
        cost_estimate=cost(8),
        name="pack_weight",
    )(bias_index, in_hbm(weight), pointwise_weight, in_hbm(gain_table.T), first)


def back_modes_kernel(
    me_ref, r0, r1, r2, r3, other_ref, x_hbm, w_ref, spread_hbm, g_ref, o_ref,
    x_ref, spread_ref, sem, g_s, b_s, t_s,
):
    copies = [
        pltpu.make_async_copy(x_hbm.at[me_ref[0]], x_ref, sem.at[0]),
        pltpu.make_async_copy(spread_hbm, spread_ref, sem.at[1]),
    ]
    for copy in copies:
        copy.start()

    def store(c, value):
        for co in range(4):
            cut = value[co * 32 : co * 32 + 32]
            g_ref[co * 8 + c] = cut.astype(BF)
            g_s[pl.ds((co * 8 + c) * 32, 32), :] = cut

    copies[0].wait()
    axial_modes(
        x_ref[...], (r0, r1, r2, r3), other_ref, spread_ref, copies[1].wait, True, store
    )

    def line(i, carry):
        g_re = g_s[pl.ds(i, 32, stride=32), :]
        g_im = g_s[pl.ds(i + 16, 32, stride=32), :]
        for c in range(32):
            w_re = w_ref[0, i, c].astype(F32)
            w_im = w_ref[1, i, c].astype(F32)
            re = w_re * g_re + w_im * g_im
            im = w_re * g_im - w_im * g_re
            t_s[0, c * 8 : c * 8 + 8, :] = (re[:8] + re[8:16]) + (re[16:24] + re[24:])
            t_s[1, c * 8 : c * 8 + 8, :] = (im[:8] + im[8:16]) + (im[16:24] + im[24:])
        for part in range(2):
            total = t_s[part, pl.ds(0, 32, stride=8), :]
            for k in range(1, 8):
                total = total + t_s[part, pl.ds(k, 32, stride=8), :]
            b_s[pl.ds(pl.multiple_of((part * 16 + i) * 32, 32), 32), :] = total * ORTHO
        return carry

    lax.fori_loop(0, M, line, 0)
    low = lax.broadcasted_iota(jnp.int32, (32, 128), 1) < 64
    stacks = [[], []]
    for co in range(4):
        cuts = [b_s[pl.ds(co * 8 + c, 32, stride=32), :] for c in range(8)]
        for a2 in range(2):
            keep = low if a2 == 0 else jnp.logical_not(low)
            stacks[a2].append(
                jnp.concatenate([jnp.where(keep, cut, 0.0).astype(BF) for cut in cuts], axis=1)
            )
    moved = lax.dot_general(
        jnp.concatenate(stacks[0] + stacks[1], axis=0),
        spread_ref[...],
        (((1,), (1,)), ((), ())),
        preferred_element_type=F32,
    ).astype(BF)
    for a2 in range(2):
        for co in range(4):
            at = (a2 * 4 + co) * 32
            o_ref[a2 * 32 : a2 * 32 + 32, co * 512 : co * 512 + 512] = moved[at : at + 32]


def back_modes(me, received, other, packed, ops):
    return pl.pallas_call(
        back_modes_kernel,
        in_specs=[SMEM] + [VMEM] * 5 + [HBM, VMEM, HBM],
        out_specs=[VMEM, VMEM],
        out_shape=[
            jax.ShapeDtypeStruct((32, 32, 128), BF),
            jax.ShapeDtypeStruct((64, 2048), BF),
        ],
        scratch_shapes=MODE_SCRATCH
        + [
            pltpu.VMEM((1024, 128), F32),
            pltpu.VMEM((1024, 128), F32),
            pltpu.VMEM((2, 256, 128), F32),
        ],
        compiler_params=params(10),
        cost_estimate=cost(6),
        name="back_modes",
    )(me, *received, other, in_hbm(ops["x"]), in_vmem(packed), in_hbm(ops["spread"]))


def planes_kernel(me_ref, b_ref, x_hbm, *rest):
    outs, (x_ref, sem) = rest[-6:-2], rest[-2:]
    copy = pltpu.make_async_copy(x_hbm.at[me_ref[0]], x_ref, sem)
    copy.start()
    copy.wait()
    table = x_ref[...].astype(F32).T.astype(BF)
    for co in range(4):
        planes = dot(table, b_ref[:, pl.ds(co * 512, 512)]).astype(BF)
        for part in range(2):
            for b in range(4):
                lane = (b * 2 + part) * 512 + co * 128
                for q in range(4):
                    outs[q][:, lane : lane + 128] = planes[
                        part * 64 + q * 16 : part * 64 + q * 16 + 16, b * 128 : b * 128 + 128
                    ]


def back_planes(me, modes, ops, first, name, ahead=()):
    return pl.pallas_call(
        planes_kernel,
        in_specs=[SMEM, VMEM, HBM, UNREAD] + [UNREAD] * len(ahead),
        out_specs=[UNREAD] + [VMEM] * 4,
        out_shape=[jax.ShapeDtypeStruct(first.shape, first.dtype)]
        + [jax.ShapeDtypeStruct((16, 4096), BF)] * 4,
        input_output_aliases={3: 0},
        scratch_shapes=[pltpu.VMEM((64, NX), BF), pltpu.SemaphoreType.DMA(())],
        compiler_params=params(16),
        cost_estimate=cost(1),
        name=name,
    )(me, modes, in_hbm(ops["x"]), first, *ahead)


def weight_grad_kernel(half_ref, u0_ref, u1_ref, g0_ref, g1_ref, o_ref, u_s, g_s):
    i = pl.program_id(0)
    lines = o_ref.shape[1] // 2

    @pl.when(i == 0)
    def _():
        for s, (u, g) in enumerate(((u0_ref, g0_ref), (u1_ref, g1_ref))):
            u_s[s] = u[...].reshape(1024, 128).astype(F32)
            g_s[s] = g[...].reshape(1024, 128).astype(F32)

    base = half_ref[0] * 512
    for k in range(lines):
        at = i * lines + k
        u = [[u_s[s, pl.ds(at + 16 * r, 32, stride=32), :] for r in range(2)] for s in range(2)]
        g = [
            [g_s[s, pl.ds(base + at + 16 * r, 16, stride=32), :] for r in range(2)]
            for s in range(2)
        ]
        for c in range(32):
            row = [
                [jnp.broadcast_to(u[s][r][c : c + 1], (16, 128)) for r in range(2)]
                for s in range(2)
            ]
            re = (row[0][0] * g[0][0] + row[0][1] * g[0][1]) + (
                row[1][0] * g[1][0] + row[1][1] * g[1][1]
            )
            im = (row[0][0] * g[0][1] - row[0][1] * g[0][0]) + (
                row[1][0] * g[1][1] - row[1][1] * g[1][0]
            )
            o_ref[0, 2 * k, c] = re[:, :64]
            o_ref[0, 2 * k + 1, c] = re[:, 64:]
            o_ref[1, 2 * k, c] = im[:, :64]
            o_ref[1, 2 * k + 1, c] = im[:, 64:]


def weight_grad(half, u0, u1, g0, g1):
    return pl.pallas_call(
        weight_grad_kernel,
        grid=(8,),
        in_specs=[SMEM] + [VMEM] * 4,
        out_specs=pl.BlockSpec((2, 4, 32, 16, 64), lambda i: (0, i, 0, 0, 0)),
        scratch_shapes=[pltpu.VMEM((2, 1024, 128), F32), pltpu.VMEM((2, 1024, 128), F32)],
        out_shape=jax.ShapeDtypeStruct((2, 32, 32, 16, 64), F32),
        compiler_params=params(16),
        cost_estimate=cost(8),
        name="weight_grad",
    )(half, u0, u1, g0, g1)


def finish_kernel(
    me_ref, n0, n1, n2, n3, f0, f1, f2, f3, v_ref, k_hbm, y_hbm, z_hbm, o_ref,
    s_ref, a_ref, i_ref, b_ref, k_ref, yt_ref, y_ref, z_ref, in_sem, out_sem, sem,
):
    received = ((n0, n1, n2, n3), (f0, f1, f2, f3))
    nx = o_ref.shape[0]
    slots = b_ref.shape[0]

    def load(x):
        slot = lax.rem(x, slots)
        return pltpu.make_async_copy(v_ref.at[x], i_ref.at[slot], in_sem.at[slot])

    def save(x):
        slot = lax.rem(x, slots)
        return pltpu.make_async_copy(b_ref.at[slot], o_ref.at[x], out_sem.at[slot])

    tables = [
        pltpu.make_async_copy(y_hbm.at[me_ref[0]], yt_ref, sem.at[0]),
        pltpu.make_async_copy(z_hbm, z_ref, sem.at[1]),
        pltpu.make_async_copy(k_hbm, k_ref, sem.at[2]),
    ]
    for table in tables:
        table.start()
    for x in range(slots - 1):
        load(x).start()
    for r in range(64):
        q, j, k = r // 16, (r // 8) % 2, r % 8
        for n in range(4):
            s_ref[n, r * 16 : r * 16 + 16, :] = received[j][q][
                :, k * 512 + n * 128 : k * 512 + n * 128 + 128
            ].astype(F32)
    for table in tables:
        table.wait()
    y_ref[...] = yt_ref[...].astype(F32).T.astype(BF)

    def one(x, carry):
        @pl.when(x + slots - 1 < nx)
        def _():
            load(x + slots - 1).start()

        @pl.when(x >= slots)
        def _():
            save(x - slots).wait()

        load(x).wait()
        slot = lax.rem(x, slots)
        planes = jnp.concatenate(
            [s_ref[n, pl.ds(x, 64, stride=16), :].astype(BF) for n in range(4)], axis=1
        )
        rows = dot(y_ref[...], planes).astype(BF)
        lhs = jnp.concatenate(
            [
                jnp.concatenate(
                    [rows[:128, co * 128 : co * 128 + 128], rows[128:, co * 128 : co * 128 + 128]],
                    axis=1,
                )
                for co in range(4)
            ],
            axis=0,
        )
        for n in range(4):
            part = dot(lhs, z_ref[:, n * 256 : n * 256 + 256])
            for co in range(4):
                for j in range(2):
                    a_ref[co * 8 + n * 2 + j] = part[
                        co * 128 : co * 128 + 128, j * 128 : j * 128 + 128
                    ]
        for y in range(8):
            cut = i_ref[slot, :, y * 16 : y * 16 + 16, :].astype(F32)
            rhs = jnp.concatenate(
                [
                    cut[:, :8].reshape(256, 128).astype(BF),
                    cut[:, 8:].reshape(256, 128).astype(BF),
                ],
                axis=1,
            )
            point = dot(k_ref[...], rhs)
            point = jnp.concatenate(
                [point[:, :128].reshape(32, 8, 128), point[:, 128:].reshape(32, 8, 128)], axis=1
            )
            b_ref[slot, :, y * 16 : y * 16 + 16, :] = (
                point + a_ref[:, y * 16 : y * 16 + 16, :]
            ).astype(BF)
        save(x).start()
        return carry

    lax.fori_loop(0, nx, one, 0)
    for x in range(nx - slots, nx):
        save(x).wait()


def finish(me, near, far, cotangent, kron, ops):
    nx = cotangent.shape[0]
    return pl.pallas_call(
        finish_kernel,
        in_specs=[SMEM] + [VMEM] * 8 + [HBM] * 4,
        out_specs=HBM,
        out_shape=jax.ShapeDtypeStruct(cotangent.shape, BF),
        scratch_shapes=[
            pltpu.VMEM((4, nx * 64, 128), F32),
            pltpu.VMEM((32, NY, NZ), F32),
            pltpu.VMEM((4, 32, NY, NZ), BF),
            pltpu.VMEM((4, 32, NY, NZ), BF),
            pltpu.VMEM((256, 256), BF),
            pltpu.VMEM((64, 256), BF),
            pltpu.VMEM((256, 64), BF),
            pltpu.VMEM((256, 1024), BF),
            pltpu.SemaphoreType.DMA((4,)),
            pltpu.SemaphoreType.DMA((4,)),
            pltpu.SemaphoreType.DMA((3,)),
        ],
        compiler_params=params(24),
        cost_estimate=cost(16),
        name="finish",
    )(
        me, *near, *far, in_hbm(cotangent), in_hbm(kron), in_hbm(ops["y"]),
        in_hbm(ops["z_back"]),
    )


ACROSS = [(s, s ^ 4) for s in range(8)]
SWAP = [(0, 1), (1, 0)]


def in_square(blocks):
    return [blocks[0]] + [
        lax.ppermute(blocks[k], "space", [(s, s ^ k) for s in range(8)]) for k in (1, 2, 3)
    ]


def tuned_device(volume, cotangent, spectral_weight, pointwise_weight, gain_table, bias_index):
    ops = fixed_operands()
    nx = volume.shape[1]
    vol = volume.reshape(nx, 32, NY, NZ)
    cot = cotangent.reshape(nx, 32, NY, NZ)
    me = lax.axis_index("space").astype(jnp.int32).reshape(1)
    half = lax.axis_index("dp").astype(jnp.int32).reshape(1)
    weight = jnp.transpose(spectral_weight, (0, 1, 3, 4, 2))

    cot_blocks = lateral(me, cot, ops, me, "cotangent_lateral")
    cot_received = in_square(cot_blocks)
    vol_blocks = lateral(me, vol, ops, cot_blocks[0], "volume_lateral")
    cot_partner, passed = partner_modes(
        me, cot_received, ops, vol_blocks[1], "cotangent_partner"
    )
    other = lax.ppermute(cot_partner, "space", ACROSS)
    vol_received = in_square([vol_blocks[0], passed, vol_blocks[2], vol_blocks[3]])
    packed, kron = pack_weight(bias_index, weight, pointwise_weight, gain_table, cot_partner)
    g_modes, back_own = back_modes(me, cot_received, other, packed, ops)
    back_other = lax.ppermute(back_own, "space", ACROSS)
    vol_partner, _ = partner_modes(me, vol_received, ops, back_own, "volume_partner")
    vol_partner, *own_planes = back_planes(me, back_own, ops, vol_partner, "own_planes")
    back_near = in_square(own_planes)
    vol_partner, *other_planes = back_planes(
        me, back_other, ops, vol_partner, "partner_planes", back_near[1:]
    )
    back_far = in_square(other_planes)
    vol_other = lax.ppermute(vol_partner, "space", ACROSS)
    u_modes = volume_modes(me, vol_received, vol_other, ops, back_far[1:])
    g_other = lax.ppermute(g_modes, "dp", SWAP)
    u_other = lax.ppermute(u_modes, "dp", SWAP)
    grad = weight_grad(half, u_modes, u_other, g_modes, g_other)
    out = finish(me, back_near, back_far, cot, kron, ops)
    return out.reshape(volume.shape), jnp.transpose(grad, (0, 1, 4, 2, 3))


def per_device(volume, cotangent, spectral_weight, pointwise_weight, gain_table, bias_index):
    fits = (
        volume.shape == (1, 16, 32, NY, NZ)
        and spectral_weight.shape == (2, 2 * M, 64, 32, 32)
        and lax.axis_size("space") == 8
        and lax.axis_size("dp") == 2
    )
    device = tuned_device if fits else general_device
    return device(
        volume, cotangent, spectral_weight, pointwise_weight, gain_table, bias_index
    )


def solution(mesh):
    return jax.shard_map(
        per_device,
        mesh=mesh,
        in_specs=(
            P(("parts", "dp"), "space", None, None, None),
            P(("parts", "dp"), "space", None, None, None),
            P(None, None, "space", None, None),
            P(),
            P(),
            P(("parts", "dp")),
        ),
        out_specs=(
            P(("parts", "dp"), "space", None, None, None),
            P("parts", None, "space", None, "dp"),
        ),
        check_vma=False,
    )
```

profile of v0, /device:TPU:0, one launch (start us, length us, event | category | flops | bytes accessed | tf_op | source)
XLA Modules:
  0.0 108.2 jit_solution(16101770983960993269)
XLA Ops:
  0.6 0.0 copy-start.1
  0.6 10.0 %cotangent_lateral.1 = (bf16[2,16,4096]{2,1,0:T(8,128)(2,1)S(1)}, bf16[2,16,4096]{2,1,0:T(8,128)(2,1)S(1)}, bf16[2,16,4096]{2,1,0:T(8,128)(2,1)S(1)}, bf16[2,16,4096]{2,1,0:T(8,128)(2,1)S(1)}) custom-call(s32[1]{0:T(128)} %bitcast.me_ref._, bf16[16,32,128,128]{3,2,1,0:T(8,128)(2,1)} %bitcast.8, bf16[1024,256]{1,0:T(8,128)(2,1)} %constant.18.clone.z_hbm, ...), custom_call_target="tpu_custom_call" | custom-call | flops 60000000 | bytes 1024 | tf_op jit(solution)/shard_map/cotangent_lateral/pallas_call | solution.py:277
  10.6 3.0 %collective-permute-start = (bf16[2,16,4096]{2,1,0:T(8,128)(2,1)S(1)}, bf16[2,16,4096]{2,1,0:T(8,128)(2,1)S(1)}, u32[]{:S(2)}, u32[]{:S(2)}) collective-permute-start(bf16[2,16,4096]{2,1,0:T(8,128)(2,1)S(1)} %get-tuple-element.28), channel_id=1, source_target_pairs={{0,2},{2,0},{4,6},{6,4},{8,10},{10,8},{12,14},{14,12},{1,3},{3,1},... | collective-permute-start | bytes 786440 | tf_op jit(solution)/shard_map/ppermute | solution.py:763
  13.6 1.6 %collective-permute-start.1 = (bf16[2,16,4096]{2,1,0:T(8,128)(2,1)S(1)}, bf16[2,16,4096]{2,1,0:T(8,128)(2,1)S(1)}, u32[]{:S(2)}, u32[]{:S(2)}) collective-permute-start(bf16[2,16,4096]{2,1,0:T(8,128)(2,1)S(1)} %get-tuple-element.29), channel_id=1, source_target_pairs={{0,4},{2,6},{4,0},{6,2},{8,12},{10,14},{12,8},{14,10},{1,5},{3,7},... | collective-permute-start | bytes 786440 | tf_op jit(solution)/shard_map/ppermute | solution.py:763
  15.2 0.0 collective-permute-start.2
  15.2 10.0 %volume_lateral.1 = (bf16[2,16,4096]{2,1,0:T(8,128)(2,1)S(1)}, bf16[2,16,4096]{2,1,0:T(8,128)(2,1)S(1)}, bf16[2,16,4096]{2,1,0:T(8,128)(2,1)S(1)}, bf16[2,16,4096]{2,1,0:T(8,128)(2,1)S(1)}) custom-call(s32[1]{0:T(128)} %bitcast.me_ref._, bf16[16,32,128,128]{3,2,1,0:T(8,128)(2,1)} %bitcast.10, bf16[1024,256]{1,0:T(8,128)(2,1)} %constant.18.clone.z_hbm, ...), custom_call_target="tpu_custom_call" | custom-call | flops 60000000 | bytes 1024 | tf_op jit(solution)/shard_map/volume_lateral/pallas_call | solution.py:277
  25.2 0.0 collective-permute-done.r1
  25.2 0.0 collective-permute-done.1.r2
  25.2 1.6 %collective-permute-done.2.r3 = bf16[2,16,4096]{2,1,0:T(8,128)(2,1)S(1)} collective-permute-done((bf16[2,16,4096]{2,1,0:T(8,128)(2,1)S(1)}, bf16[2,16,4096]{2,1,0:T(8,128)(2,1)S(1)}, u32[]{:S(2)}, u32[]{:S(2)}) %collective-permute-start.2) | collective-permute-done | bytes 262176 | tf_op jit(solution)/shard_map/ppermute | solution.py:763
  26.8 0.9 cotangent_partner.1
  27.8 2.8 %collective-permute-start.3 = (bf16[64,2048]{1,0:T(8,128)(2,1)S(1)}, bf16[64,2048]{1,0:T(8,128)(2,1)S(1)}, u32[]{:S(2)}, u32[]{:S(2)}) collective-permute-start(bf16[64,2048]{1,0:T(8,128)(2,1)S(1)} %get-tuple-element.32._), channel_id=1, source_target_pairs={{0,8},{2,10},{4,12},{6,14},{8,0},{10,2},{12,4},{14,6},{1,9},{3,11}... | collective-permute-start | bytes 786440 | tf_op jit(solution)/shard_map/ppermute | solution.py:782
  30.6 1.6 %collective-permute-start.5 = (bf16[2,16,4096]{2,1,0:T(8,128)(2,1)S(1)}, bf16[2,16,4096]{2,1,0:T(8,128)(2,1)S(1)}, u32[]{:S(2)}, u32[]{:S(2)}) collective-permute-start(bf16[2,16,4096]{2,1,0:T(8,128)(2,1)S(1)} %get-tuple-element.37), channel_id=1, source_target_pairs={{0,4},{2,6},{4,0},{6,2},{8,12},{10,14},{12,8},{14,10},{1,5},{3,7},... | collective-permute-start | bytes 786440 | tf_op jit(solution)/shard_map/ppermute | solution.py:763
  32.2 1.4 %collective-permute-start.6 = (bf16[2,16,4096]{2,1,0:T(8,128)(2,1)S(1)}, bf16[2,16,4096]{2,1,0:T(8,128)(2,1)S(1)}, u32[]{:S(2)}, u32[]{:S(2)}) collective-permute-start(bf16[2,16,4096]{2,1,0:T(8,128)(2,1)S(1)} %get-tuple-element.38), channel_id=1, source_target_pairs={{0,6},{2,4},{4,2},{6,0},{8,14},{10,12},{12,10},{14,8},{1,7},{3,5},... | collective-permute-start | bytes 786440 | tf_op jit(solution)/shard_map/ppermute | solution.py:763
  33.5 0.5 collective-permute-start.4
  34.7 0.0 copy-done.1
  34.7 7.1 %pack_weight.1 = (bf16[2,16,32,32,128]{4,3,2,1,0:T(8,128)(2,1)S(1)}, bf16[256,256]{1,0:T(8,128)(2,1)S(1)}) custom-call(s32[1]{0:T(128)S(6)} %copy.21.at_ref, bf16[2,32,32,32,64]{4,3,2,1,0:T(8,128)(2,1)} %bitcast.13, bf16[32,32]{1,0:T(8,128)(2,1)S(1)} %copy-done.1, bf16[32,4096]{1,0:T(8,128)(2,1)} %bitcast.14, bf16[64,2048]{1,0:T(8,128)(2,1)S(1)} %get-tuple-element.32._), custom_call_target="tpu_custom_call" | custom-call | flops 48000000 | bytes 1024 | tf_op jit(solution)/shard_map/pack_weight/pallas_call | solution.py:454
  41.8 0.0 copy-start
  41.8 0.0 collective-permute-done.3.other_ref
  41.8 5.7 %back_modes.1 = (bf16[32,32,128]{2,1,0:T(8,128)(2,1)S(1)}, bf16[64,2048]{1,0:T(8,128)(2,1)S(1)}) custom-call(s32[1]{0:T(128)} %bitcast.me_ref._, bf16[2,16,4096]{2,1,0:T(8,128)(2,1)S(1)} %get-tuple-element.27._.r0, bf16[2,16,4096]{2,1,0:T(8,128)(2,1)S(1)} %collective-permute-done.r1, bf16[2,16,4096]{2,1,0:T(8,128)(2,1)S(1)} %collective-permute-done.1.r2, ...), custom_call_target="tpu_custom_call" | custom-call | flops 36000000 | bytes 1024 | tf_op jit(solution)/shard_map/back_modes/pallas_call | solution.py:536
  47.6 0.2 collective-permute-start.10
  47.8 0.0 collective-permute-done.5.r2
  47.8 0.4 collective-permute-done.6.r3
  48.2 0.0 collective-permute-done.4.r1
  48.2 0.9 volume_partner.1
  49.2 1.1 own_planes.1
  50.2 1.4 %collective-permute-start.7 = (bf16[16,4096]{1,0:T(8,128)(2,1)S(1)}, bf16[16,4096]{1,0:T(8,128)(2,1)S(1)}, u32[]{:S(2)}, u32[]{:S(2)}) collective-permute-start(bf16[16,4096]{1,0:T(8,128)(2,1)S(1)} %get-tuple-element.41), channel_id=1, source_target_pairs={{0,2},{2,0},{4,6},{6,4},{8,10},{10,8},{12,14},{14,12},{1,3},{3,1},... | collective-permute-start | bytes 393224 | tf_op jit(solution)/shard_map/ppermute | solution.py:763
  51.6 3.3 %collective-permute-start.8 = (bf16[16,4096]{1,0:T(8,128)(2,1)S(1)}, bf16[16,4096]{1,0:T(8,128)(2,1)S(1)}, u32[]{:S(2)}, u32[]{:S(2)}) collective-permute-start(bf16[16,4096]{1,0:T(8,128)(2,1)S(1)} %get-tuple-element.42), channel_id=1, source_target_pairs={{0,4},{2,6},{4,0},{6,2},{8,12},{10,14},{12,8},{14,10},{1,5},{3,7},... | collective-permute-start | bytes 393224 | tf_op jit(solution)/shard_map/ppermute | solution.py:763
  54.9 0.0 collective-permute-start.9
  54.9 0.4 collective-permute-done.7.rest_1_.n1
  55.3 7.5 %collective-permute-done.8.rest_2_.n2 = bf16[16,4096]{1,0:T(8,128)(2,1)S(1)} collective-permute-done((bf16[16,4096]{1,0:T(8,128)(2,1)S(1)}, bf16[16,4096]{1,0:T(8,128)(2,1)S(1)}, u32[]{:S(2)}, u32[]{:S(2)}) %collective-permute-start.8) | collective-permute-done | bytes 131104 | tf_op jit(solution)/shard_map/ppermute | solution.py:763
  62.8 1.5 %collective-permute-done.9.rest_3_.n3 = bf16[16,4096]{1,0:T(8,128)(2,1)S(1)} collective-permute-done((bf16[16,4096]{1,0:T(8,128)(2,1)S(1)}, bf16[16,4096]{1,0:T(8,128)(2,1)S(1)}, u32[]{:S(2)}, u32[]{:S(2)}) %collective-permute-start.9) | collective-permute-done | bytes 131104 | tf_op jit(solution)/shard_map/ppermute | solution.py:763
  64.3 0.0 collective-permute-done.10.b_ref
  64.3 1.1 partner_planes.1
  65.4 1.6 %collective-permute-start.14 = (bf16[64,2048]{1,0:T(8,128)(2,1)S(1)}, bf16[64,2048]{1,0:T(8,128)(2,1)S(1)}, u32[]{:S(2)}, u32[]{:S(2)}) collective-permute-start(bf16[64,2048]{1,0:T(8,128)(2,1)S(1)} %get-tuple-element.50), channel_id=1, source_target_pairs={{0,8},{2,10},{4,12},{6,14},{8,0},{10,2},{12,4},{14,6},{1,9},{3,11}... | collective-permute-start | bytes 786440 | tf_op jit(solution)/shard_map/ppermute | solution.py:794
  67.0 0.5 collective-permute-start.11
  67.6 3.4 %collective-permute-start.12 = (bf16[16,4096]{1,0:T(8,128)(2,1)S(1)}, bf16[16,4096]{1,0:T(8,128)(2,1)S(1)}, u32[]{:S(2)}, u32[]{:S(2)}) collective-permute-start(bf16[16,4096]{1,0:T(8,128)(2,1)S(1)} %get-tuple-element.47), channel_id=1, source_target_pairs={{0,4},{2,6},{4,0},{6,2},{8,12},{10,14},{12,8},{14,10},{1,5},{3,7},... | collective-permute-start | bytes 393224 | tf_op jit(solution)/shard_map/ppermute | solution.py:763
  71.0 0.0 collective-permute-start.13
  71.0 0.0 collective-permute-start.16
  71.0 1.1 collective-permute-done.11.f1.rest_0_
  72.0 8.1 %collective-permute-done.12.f2.rest_1_ = bf16[16,4096]{1,0:T(8,128)(2,1)S(1)} collective-permute-done((bf16[16,4096]{1,0:T(8,128)(2,1)S(1)}, bf16[16,4096]{1,0:T(8,128)(2,1)S(1)}, u32[]{:S(2)}, u32[]{:S(2)}) %collective-permute-start.12) | collective-permute-done | bytes 131104 | tf_op jit(solution)/shard_map/ppermute | solution.py:763
  80.2 1.0 collective-permute-done.13.f3.rest_2_
  81.2 0.0 collective-permute-done.14.other_ref
  81.2 1.7 %volume_modes.1.u0_ref = bf16[32,32,128]{2,1,0:T(8,128)(2,1)S(1)} custom-call(s32[1]{0:T(128)} %bitcast.me_ref._, bf16[2,16,4096]{2,1,0:T(8,128)(2,1)S(1)} %get-tuple-element.35.r0, bf16[2,16,4096]{2,1,0:T(8,128)(2,1)S(1)} %collective-permute-done.4.r1, bf16[2,16,4096]{2,1,0:T(8,128)(2,1)S(1)} %collective-permute-done.5.r2, ...), custom_call_target="tpu_custom_call" | custom-call | flops 9000000 | bytes 1024 | tf_op jit(solution)/shard_map/volume_modes/pallas_call | solution.py:386
  82.9 0.0 copy-done
  82.9 0.1 collective-permute-start.15
  83.0 17.3 %finish.1 = bf16[16,32,128,128]{3,2,1,0:T(8,128)(2,1)} custom-call(s32[1]{0:T(128)} %bitcast.me_ref._, bf16[16,4096]{1,0:T(8,128)(2,1)S(1)} %get-tuple-element.40.n0, bf16[16,4096]{1,0:T(8,128)(2,1)S(1)} %collective-permute-done.7.rest_1_.n1, bf16[16,4096]{1,0:T(8,128)(2,1)S(1)} %collective-permute-done.8.rest_2_.n2, ...), custom_call_target="tpu_custom_call" | custom-call | flops 96000000 | bytes 1024 | tf_op jit(solution)/shard_map/finish/pallas_call | solution.py:730
  100.3 0.0 collective-permute-done.16.g1_ref
  100.3 0.0 collective-permute-done.15.u1_ref
  100.3 7.8 %weight_grad.1 = f32[2,32,32,16,64]{4,3,2,1,0:T(8,128)} custom-call(s32[1]{0:T(128)} %bitcast.6.half_ref, bf16[32,32,128]{2,1,0:T(8,128)(2,1)S(1)} %volume_modes.1.u0_ref, bf16[32,32,128]{2,1,0:T(8,128)(2,1)S(1)} %collective-permute-done.15.u1_ref, bf16[32,32,128]{2,1,0:T(8,128)(2,1)S(1)} %get-tuple-element.51.g0_ref, ...), custom_call_target="tpu_custom_call" | custom-call | flops 48000000 | bytes 1024 | tf_op jit(solution)/shard_map/weight_grad/pallas_call | solution.py:624
  (1 shorter events, 0.0 us)
Async XLA Ops:
  0.6 34.1 %copy-start.1 = (bf16[32,32]{1,0:T(8,128)(2,1)S(1)}, bf16[32,32]{1,0:T(8,128)(2,1)}, u32[]{:S(2)}) copy-start(bf16[32,32]{1,0:T(8,128)(2,1)} %p_ref.1) | copy-start | bytes 6148
  10.6 14.6 %collective-permute-start = (bf16[2,16,4096]{2,1,0:T(8,128)(2,1)S(1)}, bf16[2,16,4096]{2,1,0:T(8,128)(2,1)S(1)}, u32[]{:S(2)}, u32[]{:S(2)}) collective-permute-start(bf16[2,16,4096]{2,1,0:T(8,128)(2,1)S(1)} %get-tuple-element.28), channel_id=1, source_target_pairs={{0,2},{2,0},{4,6},{6,4},{8,10},{10,8},{12,14},{14,12},{1,3},{3,1},... | collective-permute-start | bytes 786440 | tf_op jit(solution)/shard_map/ppermute | solution.py:763
  13.6 11.6 %collective-permute-start.1 = (bf16[2,16,4096]{2,1,0:T(8,128)(2,1)S(1)}, bf16[2,16,4096]{2,1,0:T(8,128)(2,1)S(1)}, u32[]{:S(2)}, u32[]{:S(2)}) collective-permute-start(bf16[2,16,4096]{2,1,0:T(8,128)(2,1)S(1)} %get-tuple-element.29), channel_id=1, source_target_pairs={{0,4},{2,6},{4,0},{6,2},{8,12},{10,14},{12,8},{14,10},{1,5},{3,7},... | collective-permute-start | bytes 786440 | tf_op jit(solution)/shard_map/ppermute | solution.py:763
  15.2 11.6 %collective-permute-start.2 = (bf16[2,16,4096]{2,1,0:T(8,128)(2,1)S(1)}, bf16[2,16,4096]{2,1,0:T(8,128)(2,1)S(1)}, u32[]{:S(2)}, u32[]{:S(2)}) collective-permute-start(bf16[2,16,4096]{2,1,0:T(8,128)(2,1)S(1)} %get-tuple-element.30), channel_id=1, source_target_pairs={{0,6},{2,4},{4,2},{6,0},{8,14},{10,12},{12,10},{14,8},{1,7},{3,5},... | collective-permute-start | bytes 786440 | tf_op jit(solution)/shard_map/ppermute | solution.py:763
  27.8 14.1 %collective-permute-start.3 = (bf16[64,2048]{1,0:T(8,128)(2,1)S(1)}, bf16[64,2048]{1,0:T(8,128)(2,1)S(1)}, u32[]{:S(2)}, u32[]{:S(2)}) collective-permute-start(bf16[64,2048]{1,0:T(8,128)(2,1)S(1)} %get-tuple-element.32._), channel_id=1, source_target_pairs={{0,8},{2,10},{4,12},{6,14},{8,0},{10,2},{12,4},{14,6},{1,9},{3,11}... | collective-permute-start | bytes 786440 | tf_op jit(solution)/shard_map/ppermute | solution.py:782
  30.6 17.2 %collective-permute-start.5 = (bf16[2,16,4096]{2,1,0:T(8,128)(2,1)S(1)}, bf16[2,16,4096]{2,1,0:T(8,128)(2,1)S(1)}, u32[]{:S(2)}, u32[]{:S(2)}) collective-permute-start(bf16[2,16,4096]{2,1,0:T(8,128)(2,1)S(1)} %get-tuple-element.37), channel_id=1, source_target_pairs={{0,4},{2,6},{4,0},{6,2},{8,12},{10,14},{12,8},{14,10},{1,5},{3,7},... | collective-permute-start | bytes 786440 | tf_op jit(solution)/shard_map/ppermute | solution.py:763
  32.2 16.0 %collective-permute-start.6 = (bf16[2,16,4096]{2,1,0:T(8,128)(2,1)S(1)}, bf16[2,16,4096]{2,1,0:T(8,128)(2,1)S(1)}, u32[]{:S(2)}, u32[]{:S(2)}) collective-permute-start(bf16[2,16,4096]{2,1,0:T(8,128)(2,1)S(1)} %get-tuple-element.38), channel_id=1, source_target_pairs={{0,6},{2,4},{4,2},{6,0},{8,14},{10,12},{12,10},{14,8},{1,7},{3,5},... | collective-permute-start | bytes 786440 | tf_op jit(solution)/shard_map/ppermute | solution.py:763
  33.5 14.7 %collective-permute-start.4 = (bf16[2,16,4096]{2,1,0:T(8,128)(2,1)S(1)}, bf16[2,16,4096]{2,1,0:T(8,128)(2,1)S(1)}, u32[]{:S(2)}, u32[]{:S(2)}) collective-permute-start(bf16[2,16,4096]{2,1,0:T(8,128)(2,1)S(1)} %get-tuple-element.36), channel_id=1, source_target_pairs={{0,2},{2,0},{4,6},{6,4},{8,10},{10,8},{12,14},{14,12},{1,3},{3,1},... | collective-permute-start | bytes 786440 | tf_op jit(solution)/shard_map/ppermute | solution.py:763
  41.8 41.1 %copy-start = (bf16[256,256]{1,0:T(8,128)(2,1)}, bf16[256,256]{1,0:T(8,128)(2,1)S(1)}, u32[]{:S(2)}) copy-start(bf16[256,256]{1,0:T(8,128)(2,1)S(1)} %get-tuple-element.49.k_hbm) | copy-start | bytes 393220
  47.6 16.8 %collective-permute-start.10 = (bf16[64,2048]{1,0:T(8,128)(2,1)S(1)}, bf16[64,2048]{1,0:T(8,128)(2,1)S(1)}, u32[]{:S(2)}, u32[]{:S(2)}) collective-permute-start(bf16[64,2048]{1,0:T(8,128)(2,1)S(1)} %get-tuple-element.34.b_ref), channel_id=1, source_target_pairs={{0,8},{2,10},{4,12},{6,14},{8,0},{10,2},{12,4},{14,6},{1,9},{3,11}... | collective-permute-start | bytes 786440 | tf_op jit(solution)/shard_map/ppermute | solution.py:786
  50.2 5.0 %collective-permute-start.7 = (bf16[16,4096]{1,0:T(8,128)(2,1)S(1)}, bf16[16,4096]{1,0:T(8,128)(2,1)S(1)}, u32[]{:S(2)}, u32[]{:S(2)}) collective-permute-start(bf16[16,4096]{1,0:T(8,128)(2,1)S(1)} %get-tuple-element.41), channel_id=1, source_target_pairs={{0,2},{2,0},{4,6},{6,4},{8,10},{10,8},{12,14},{14,12},{1,3},{3,1},... | collective-permute-start | bytes 393224 | tf_op jit(solution)/shard_map/ppermute | solution.py:763
  51.6 11.2 %collective-permute-start.8 = (bf16[16,4096]{1,0:T(8,128)(2,1)S(1)}, bf16[16,4096]{1,0:T(8,128)(2,1)S(1)}, u32[]{:S(2)}, u32[]{:S(2)}) collective-permute-start(bf16[16,4096]{1,0:T(8,128)(2,1)S(1)} %get-tuple-element.42), channel_id=1, source_target_pairs={{0,4},{2,6},{4,0},{6,2},{8,12},{10,14},{12,8},{14,10},{1,5},{3,7},... | collective-permute-start | bytes 393224 | tf_op jit(solution)/shard_map/ppermute | solution.py:763
  54.9 9.4 %collective-permute-start.9 = (bf16[16,4096]{1,0:T(8,128)(2,1)S(1)}, bf16[16,4096]{1,0:T(8,128)(2,1)S(1)}, u32[]{:S(2)}, u32[]{:S(2)}) collective-permute-start(bf16[16,4096]{1,0:T(8,128)(2,1)S(1)} %get-tuple-element.43), channel_id=1, source_target_pairs={{0,6},{2,4},{4,2},{6,0},{8,14},{10,12},{12,10},{14,8},{1,7},{3,5},... | collective-permute-start | bytes 393224 | tf_op jit(solution)/shard_map/ppermute | solution.py:763
  65.4 15.7 %collective-permute-start.14 = (bf16[64,2048]{1,0:T(8,128)(2,1)S(1)}, bf16[64,2048]{1,0:T(8,128)(2,1)S(1)}, u32[]{:S(2)}, u32[]{:S(2)}) collective-permute-start(bf16[64,2048]{1,0:T(8,128)(2,1)S(1)} %get-tuple-element.50), channel_id=1, source_target_pairs={{0,8},{2,10},{4,12},{6,14},{8,0},{10,2},{12,4},{14,6},{1,9},{3,11}... | collective-permute-start | bytes 786440 | tf_op jit(solution)/shard_map/ppermute | solution.py:794
  67.0 5.0 %collective-permute-start.11 = (bf16[16,4096]{1,0:T(8,128)(2,1)S(1)}, bf16[16,4096]{1,0:T(8,128)(2,1)S(1)}, u32[]{:S(2)}, u32[]{:S(2)}) collective-permute-start(bf16[16,4096]{1,0:T(8,128)(2,1)S(1)} %get-tuple-element.46), channel_id=1, source_target_pairs={{0,2},{2,0},{4,6},{6,4},{8,10},{10,8},{12,14},{14,12},{1,3},{3,1},... | collective-permute-start | bytes 393224 | tf_op jit(solution)/shard_map/ppermute | solution.py:763
  67.6 12.6 %collective-permute-start.12 = (bf16[16,4096]{1,0:T(8,128)(2,1)S(1)}, bf16[16,4096]{1,0:T(8,128)(2,1)S(1)}, u32[]{:S(2)}, u32[]{:S(2)}) collective-permute-start(bf16[16,4096]{1,0:T(8,128)(2,1)S(1)} %get-tuple-element.47), channel_id=1, source_target_pairs={{0,4},{2,6},{4,0},{6,2},{8,12},{10,14},{12,8},{14,10},{1,5},{3,7},... | collective-permute-start | bytes 393224 | tf_op jit(solution)/shard_map/ppermute | solution.py:763
  71.0 10.2 %collective-permute-start.13 = (bf16[16,4096]{1,0:T(8,128)(2,1)S(1)}, bf16[16,4096]{1,0:T(8,128)(2,1)S(1)}, u32[]{:S(2)}, u32[]{:S(2)}) collective-permute-start(bf16[16,4096]{1,0:T(8,128)(2,1)S(1)} %get-tuple-element.48), channel_id=1, source_target_pairs={{0,6},{2,4},{4,2},{6,0},{8,14},{10,12},{12,10},{14,8},{1,7},{3,5},... | collective-permute-start | bytes 393224 | tf_op jit(solution)/shard_map/ppermute | solution.py:763
  71.0 29.3 %collective-permute-start.16 = (bf16[32,32,128]{2,1,0:T(8,128)(2,1)S(1)}, bf16[32,32,128]{2,1,0:T(8,128)(2,1)S(1)}, u32[]{:S(2)}, u32[]{:S(2)}) collective-permute-start(bf16[32,32,128]{2,1,0:T(8,128)(2,1)S(1)} %get-tuple-element.51.g0_ref), channel_id=1, source_target_pairs={{0,1},{1,0},{2,3},{3,2},{4,5},{5,4},{6,7},{7,6},{8,9},{9,8},{10,11... | collective-permute-start | bytes 786440 | tf_op jit(solution)/shard_map/ppermute | solution.py:796
  82.9 17.4 %collective-permute-start.15 = (bf16[32,32,128]{2,1,0:T(8,128)(2,1)S(1)}, bf16[32,32,128]{2,1,0:T(8,128)(2,1)S(1)}, u32[]{:S(2)}, u32[]{:S(2)}) collective-permute-start(bf16[32,32,128]{2,1,0:T(8,128)(2,1)S(1)} %volume_modes.1.u0_ref), channel_id=1, source_target_pairs={{0,1},{1,0},{2,3},{3,2},{4,5},{5,4},{6,7},{7,6},{8,9},{9,8},{10,11... | collective-permute-start | bytes 786440 | tf_op jit(solution)/shard_map/ppermute | solution.py:797
where the time goes:
time: 109 us; the launch traced here: 108 us
  Pallas kernels  63.6 us (58%)
  waiting for transfers between devices  21.6 us (20%)
  starting transfers between devices  21.4 us (20%)
  between operations  1.47 us (1%)
    ppermute x12, waiting for transfers between devices, in_square(): lax.ppermute(blocks[k], 'space', [(s, s ^ k) for s in range(8)])  21.6 us
    pallas_call x2, Pallas kernels, lateral(): pl.pallas_call(lateral_kernel, in_specs=[SMEM, HBM, HBM, HBM, UNREAD], ou...  19.9 us
    pallas_call x1, Pallas kernels, finish(): pl.pallas_call(finish_kernel, in_specs=[SMEM] + [VMEM] * 8 + [HBM] * 4, o...  17.3 us
    ppermute x12, starting transfers between devices, in_square(): lax.ppermute(blocks[k], 'space', [(s, s ^ k) for s in range(8)])  16.7 us
    pallas_call x1, Pallas kernels, weight_grad(): pl.pallas_call(weight_grad_kernel, grid=(8,), in_specs=[SMEM] + [VMEM] *...  7.83 us
    pallas_call x1, Pallas kernels, pack_weight(): pl.pallas_call(pack_kernel, in_specs=[SMEM, HBM, VMEM, HBM, UNREAD], out_...  7.07 us
    pallas_call x1, Pallas kernels, back_modes(): pl.pallas_call(back_modes_kernel, in_specs=[SMEM] + [VMEM] * 5 + [HBM, VM...  5.71 us
    ppermute x1, starting transfers between devices, tuned_device(): other = lax.ppermute(cot_partner, 'space', ACROSS)  2.82 us
  transfers between devices with their start and end apart: 17, of which 8 were waited for; matrix products, arithmetic and copies ran while one was open for 0% of the time, Pallas kernels for 40%

commit v1 on v0

--- a/solution.py
+++ b/solution.py
@@ -385,7 +385,7 @@
 def volume_modes(me, received, other, ops, ahead):
     return pl.pallas_call(
         volume_modes_kernel,
-        in_specs=[SMEM] + [VMEM] * 5 + [HBM] * 2 + [UNREAD] * len(ahead),
+        in_specs=[SMEM] + [VMEM] * 5 + [HBM] * 2 + [HBM] * len(ahead),
         out_specs=VMEM,
         out_shape=jax.ShapeDtypeStruct((32, 32, 128), BF),
         scratch_shapes=MODE_SCRATCH,
@@ -457,7 +457,7 @@
         out_specs=[VMEM, VMEM],
         out_shape=[
             pltpu.VMEM((2, M, 32, 32, 128), BF),
-            jax.ShapeDtypeStruct((256, 256), BF),
+            pltpu.HBM((256, 256), BF),
         ],
         scratch_shapes=[
             pltpu.VMEM((9, 2, 2, 32, 32, 64), BF),
@@ -570,10 +570,10 @@
                     ]
 
 
-def back_planes(me, modes, ops, first, name, ahead=()):
+def back_planes(me, modes, ops, first, name, ahead=(), far=()):
     return pl.pallas_call(
         planes_kernel,
-        in_specs=[SMEM, VMEM, HBM, UNREAD] + [UNREAD] * len(ahead),
+        in_specs=[SMEM, VMEM, HBM, UNREAD] + [UNREAD] * len(ahead) + [HBM] * len(far),
         out_specs=[UNREAD] + [VMEM] * 4,
         out_shape=[jax.ShapeDtypeStruct(first.shape, first.dtype)]
         + [jax.ShapeDtypeStruct((16, 4096), BF)] * 4,
@@ -582,7 +582,7 @@
         compiler_params=params(16),
         cost_estimate=cost(1),
         name=name,
-    )(me, modes, in_hbm(ops["x"]), first, *ahead)
+    )(me, modes, in_hbm(ops["x"]), first, *ahead, *[in_hbm(x) for x in far])
 
 
 def weight_grad_kernel(half_ref, u0_ref, u1_ref, g0_ref, g1_ref, o_ref, u_s, g_s):
@@ -623,9 +623,9 @@
 def weight_grad(half, u0, u1, g0, g1):
     return pl.pallas_call(
         weight_grad_kernel,
-        grid=(8,),
+        grid=(4,),
         in_specs=[SMEM] + [VMEM] * 4,
-        out_specs=pl.BlockSpec((2, 4, 32, 16, 64), lambda i: (0, i, 0, 0, 0)),
+        out_specs=pl.BlockSpec((2, 8, 32, 16, 64), lambda i: (0, i, 0, 0, 0)),
         scratch_shapes=[pltpu.VMEM((2, 1024, 128), F32), pltpu.VMEM((2, 1024, 128), F32)],
         out_shape=jax.ShapeDtypeStruct((2, 32, 32, 16, 64), F32),
         compiler_params=params(16),
@@ -634,31 +634,148 @@
     )(half, u0, u1, g0, g1)
 
 
+def pointwise_kernel(base, v_ref, k_hbm, _, o_ref, __, k_ref, i_ref, in_sem, k_sem):
+    nx = o_ref.shape[0]
+    slots = i_ref.shape[0]
+
+    def load(x):
+        slot = lax.rem(x, slots)
+        return pltpu.make_async_copy(v_ref.at[base + x], i_ref.at[slot], in_sem.at[slot])
+
+    table = pltpu.make_async_copy(k_hbm, k_ref, k_sem)
+    table.start()
+    for x in range(slots - 1):
+        load(x).start()
+    table.wait()
+
+    def one(x, carry):
+        @pl.when(x + slots - 1 < nx)
+        def _():
+            load(x + slots - 1).start()
+
+        load(x).wait()
+        slot = lax.rem(x, slots)
+        for y in range(8):
+            cut = i_ref[slot, :, y * 16 : y * 16 + 16, :].astype(F32)
+            rhs = jnp.concatenate(
+                [
+                    cut[:, :8].reshape(256, 128).astype(BF),
+                    cut[:, 8:].reshape(256, 128).astype(BF),
+                ],
+                axis=1,
+            )
+            point = dot(k_ref[...], rhs)
+            o_ref[x, :, y * 16 : y * 16 + 16, :] = jnp.concatenate(
+                [point[:, :128].reshape(32, 8, 128), point[:, 128:].reshape(32, 8, 128)], axis=1
+            ).astype(BF)
+        return carry
+
+    lax.fori_loop(0, nx, one, 0)
+
+
+def pointwise_save_kernel(base, v_ref, k_hbm, _, o_hbm, __, b_ref, out_sem, *scratch):
+    k_ref, i_ref, in_sem, k_sem = scratch
+    nx = o_hbm.shape[0]
+    slots = i_ref.shape[0]
+
+    def load(x):
+        slot = lax.rem(x, slots)
+        return pltpu.make_async_copy(v_ref.at[base + x], i_ref.at[slot], in_sem.at[slot])
+
+    def save(x):
+        slot = lax.rem(x, slots)
+        return pltpu.make_async_copy(b_ref.at[slot], o_hbm.at[x], out_sem.at[slot])
+
+    table = pltpu.make_async_copy(k_hbm, k_ref, k_sem)
+    table.start()
+    for x in range(slots - 1):
+        load(x).start()
+    table.wait()
+
+    def one(x, carry):
+        @pl.when(x + slots - 1 < nx)
+        def _():
+            load(x + slots - 1).start()
+
+        @pl.when(x >= slots)
+        def _():
+            save(x - slots).wait()
+
+        load(x).wait()
+        slot = lax.rem(x, slots)
+        for y in range(8):
+            cut = i_ref[slot, :, y * 16 : y * 16 + 16, :].astype(F32)
+            rhs = jnp.concatenate(
+                [
+                    cut[:, :8].reshape(256, 128).astype(BF),
+                    cut[:, 8:].reshape(256, 128).astype(BF),
+                ],
+                axis=1,
+            )
+            point = dot(k_ref[...], rhs)
+            b_ref[slot, :, y * 16 : y * 16 + 16, :] = jnp.concatenate(
+                [point[:, :128].reshape(32, 8, 128), point[:, 128:].reshape(32, 8, 128)], axis=1
+            ).astype(BF)
+        save(x).start()
+        return carry
+
+    lax.fori_loop(0, nx, one, 0)
+    for x in range(nx - slots, nx):
+        save(x).wait()
+
+
+def pointwise(cotangent, kron, base, count, first, keep, name):
+    shape = (count, 32, NY, NZ)
+    scratch = [
+        pltpu.VMEM((256, 256), BF),
+        pltpu.VMEM((4, 32, NY, NZ), BF),
+        pltpu.SemaphoreType.DMA((4,)),
+        pltpu.SemaphoreType.DMA(()),
+    ]
+    if not keep:
+        scratch = [pltpu.VMEM((4, 32, NY, NZ), BF), pltpu.SemaphoreType.DMA((4,))] + scratch
+    return pl.pallas_call(
+        functools.partial(pointwise_kernel if keep else pointwise_save_kernel, base),
+        in_specs=[HBM, HBM, UNREAD],
+        out_specs=[VMEM if keep else HBM, UNREAD],
+        out_shape=[
+            pltpu.VMEM(shape, BF) if keep else pltpu.HBM(shape, BF),
+            jax.ShapeDtypeStruct(first.shape, first.dtype),
+        ],
+        input_output_aliases={2: 1},
+        scratch_shapes=scratch,
+        compiler_params=params(12),
+        cost_estimate=cost(5),
+        name=name,
+    )(in_hbm(cotangent), in_hbm(kron), first)
+
+
 def finish_kernel(
-    me_ref, n0, n1, n2, n3, f0, f1, f2, f3, v_ref, k_hbm, y_hbm, z_hbm, o_ref,
-    s_ref, a_ref, i_ref, b_ref, k_ref, yt_ref, y_ref, z_ref, in_sem, out_sem, sem,
+    me_ref, n0, n1, n2, n3, f0, f1, f2, f3, p_ref, q_ref, y_hbm, z_hbm, o_ref,
+    s_ref, i_ref, b_ref, yt_ref, y_ref, z_ref, in_sem, out_sem, sem,
 ):
     received = ((n0, n1, n2, n3), (f0, f1, f2, f3))
-    nx = o_ref.shape[0]
+    split = p_ref.shape[0]
+    total = o_ref.shape[0]
     slots = b_ref.shape[0]
 
     def load(x):
-        slot = lax.rem(x, slots)
-        return pltpu.make_async_copy(v_ref.at[x], i_ref.at[slot], in_sem.at[slot])
-
-    def save(x):
-        slot = lax.rem(x, slots)
-        return pltpu.make_async_copy(b_ref.at[slot], o_ref.at[x], out_sem.at[slot])
+        slot = lax.rem(x, i_ref.shape[0])
+        return pltpu.make_async_copy(p_ref.at[x], i_ref.at[slot], in_sem.at[slot])
+
+    def place(t):
+        return lax.rem(t + split, total)
+
+    def save(t):
+        slot = lax.rem(t, slots)
+        return pltpu.make_async_copy(b_ref.at[slot], o_ref.at[place(t)], out_sem.at[slot])
 
     tables = [
         pltpu.make_async_copy(y_hbm.at[me_ref[0]], yt_ref, sem.at[0]),
         pltpu.make_async_copy(z_hbm, z_ref, sem.at[1]),
-        pltpu.make_async_copy(k_hbm, k_ref, sem.at[2]),
     ]
     for table in tables:
         table.start()
-    for x in range(slots - 1):
-        load(x).start()
     for r in range(64):
         q, j, k = r // 16, (r // 8) % 2, r % 8
         for n in range(4):
@@ -668,18 +785,16 @@
     for table in tables:
         table.wait()
     y_ref[...] = yt_ref[...].astype(F32).T.astype(BF)
-
-    def one(x, carry):
-        @pl.when(x + slots - 1 < nx)
+    for x in range(i_ref.shape[0]):
+        load(x).start()
+
+    def step(t, point):
+        @pl.when(t >= slots)
         def _():
-            load(x + slots - 1).start()
-
-        @pl.when(x >= slots)
-        def _():
-            save(x - slots).wait()
-
-        load(x).wait()
-        slot = lax.rem(x, slots)
+            save(t - slots).wait()
+
+        x = place(t)
+        slot = lax.rem(t, slots)
         planes = jnp.concatenate(
             [s_ref[n, pl.ds(x, 64, stride=16), :].astype(BF) for n in range(4)], axis=1
         )
@@ -698,59 +813,57 @@
             part = dot(lhs, z_ref[:, n * 256 : n * 256 + 256])
             for co in range(4):
                 for j in range(2):
-                    a_ref[co * 8 + n * 2 + j] = part[
-                        co * 128 : co * 128 + 128, j * 128 : j * 128 + 128
-                    ]
-        for y in range(8):
-            cut = i_ref[slot, :, y * 16 : y * 16 + 16, :].astype(F32)
-            rhs = jnp.concatenate(
-                [
-                    cut[:, :8].reshape(256, 128).astype(BF),
-                    cut[:, 8:].reshape(256, 128).astype(BF),
-                ],
-                axis=1,
-            )
-            point = dot(k_ref[...], rhs)
-            point = jnp.concatenate(
-                [point[:, :128].reshape(32, 8, 128), point[:, 128:].reshape(32, 8, 128)], axis=1
-            )
-            b_ref[slot, :, y * 16 : y * 16 + 16, :] = (
-                point + a_ref[:, y * 16 : y * 16 + 16, :]
-            ).astype(BF)
-        save(x).start()
+                    c = co * 8 + n * 2 + j
+                    b_ref[slot, c] = (
+                        part[co * 128 : co * 128 + 128, j * 128 : j * 128 + 128]
+                        + point[c].astype(F32)
+                    ).astype(BF)
+        save(t).start()
+
+    def kept(t, carry):
+        step(t, q_ref.at[t])
         return carry
 
-    lax.fori_loop(0, nx, one, 0)
-    for x in range(nx - slots, nx):
-        save(x).wait()
-
-
-def finish(me, near, far, cotangent, kron, ops):
-    nx = cotangent.shape[0]
+    def loaded(x, carry):
+        load(x).wait()
+        step(x + total - split, i_ref.at[lax.rem(x, i_ref.shape[0])])
+
+        @pl.when(x + i_ref.shape[0] < split)
+        def _():
+            load(x + i_ref.shape[0]).start()
+
+        return carry
+
+    lax.fori_loop(0, total - split, kept, 0)
+    lax.fori_loop(0, split, loaded, 0)
+    for t in range(total - slots, total):
+        save(t).wait()
+
+
+def finish(me, near, far, saved, kept, ops):
+    nx = saved.shape[0] + kept.shape[0]
+    shape = (nx,) + saved.shape[1:]
     return pl.pallas_call(
         finish_kernel,
-        in_specs=[SMEM] + [VMEM] * 8 + [HBM] * 4,
+        in_specs=[SMEM] + [VMEM] * 8 + [HBM, VMEM, HBM, HBM],
         out_specs=HBM,
-        out_shape=jax.ShapeDtypeStruct(cotangent.shape, BF),
+        out_shape=jax.ShapeDtypeStruct(shape, BF),
         scratch_shapes=[
             pltpu.VMEM((4, nx * 64, 128), F32),
-            pltpu.VMEM((32, NY, NZ), F32),
             pltpu.VMEM((4, 32, NY, NZ), BF),
             pltpu.VMEM((4, 32, NY, NZ), BF),
-            pltpu.VMEM((256, 256), BF),
             pltpu.VMEM((64, 256), BF),
             pltpu.VMEM((256, 64), BF),
             pltpu.VMEM((256, 1024), BF),
             pltpu.SemaphoreType.DMA((4,)),
             pltpu.SemaphoreType.DMA((4,)),
-            pltpu.SemaphoreType.DMA((3,)),
+            pltpu.SemaphoreType.DMA((2,)),
         ],
-        compiler_params=params(24),
-        cost_estimate=cost(16),
+        compiler_params=params(16),
+        cost_estimate=cost(12),
         name="finish",
     )(
-        me, *near, *far, in_hbm(cotangent), in_hbm(kron), in_hbm(ops["y"]),
-        in_hbm(ops["z_back"]),
+        me, *near, *far, in_hbm(saved), in_vmem(kept), in_hbm(ops["y"]), in_hbm(ops["z_back"])
     )
 
 
@@ -787,16 +900,22 @@
     vol_partner, _ = partner_modes(me, vol_received, ops, back_own, "volume_partner")
     vol_partner, *own_planes = back_planes(me, back_own, ops, vol_partner, "own_planes")
     back_near = in_square(own_planes)
+    saved, back_near[0] = pointwise(
+        cot, kron, 0, nx // 2, own_planes[0], False, "pointwise_first"
+    )
     vol_partner, *other_planes = back_planes(
-        me, back_other, ops, vol_partner, "partner_planes", back_near[1:]
+        me, back_other, ops, vol_partner, "partner_planes", back_near[1:], [saved]
     )
     back_far = in_square(other_planes)
+    kept, back_far[0] = pointwise(
+        cot, kron, nx // 2, nx - nx // 2, other_planes[0], True, "pointwise_second"
+    )
     vol_other = lax.ppermute(vol_partner, "space", ACROSS)
-    u_modes = volume_modes(me, vol_received, vol_other, ops, back_far[1:])
+    out = finish(me, back_near, back_far, saved, kept, ops)
+    u_modes = volume_modes(me, vol_received, vol_other, ops, [in_hbm(out)])
     g_other = lax.ppermute(g_modes, "dp", SWAP)
     u_other = lax.ppermute(u_modes, "dp", SWAP)
     grad = weight_grad(half, u_modes, u_other, g_modes, g_other)
-    out = finish(me, back_near, back_far, cot, kron, ops)
     return out.reshape(volume.shape), jnp.transpose(grad, (0, 1, 4, 2, 3))
 
 

time: 109 us -> 105 us (0.963)
  waiting for transfers between devices: 21.6 us -> 10.1 us
  Pallas kernels: 63.6 us -> 71.1 us
    ppermute x12, waiting for transfers between devices: 21.6 us -> 8.62 us  [in_square(): lax.ppermute(blocks[k], 'space', [(s, s ^ k) for s in range(8)])]
    pallas_call x2 -> x4, Pallas kernels: 25.2 us -> 32.2 us  [the longest x2 12.8 us: pointwise(): pl.pallas_call(functools.partial(pointwise_kernel if keep else pointwise_...]
    ppermute x1, waiting for transfers between devices: 0.01 us -> 1.51 us  [tuned_device(): u_other = lax.ppermute(u_modes, 'dp', SWAP)]
  transfers between devices with their start and end apart: 17 -> 17, of which waited for: 8 -> 5; matrix products, arithmetic and copies ran while one was open for 0% -> 0% of each run, Pallas kernels for 40% -> 50%
where the time goes in v1:
time: 105 us; the launch traced here: 104 us
  Pallas kernels  71.1 us (68%)
  starting transfers between devices  21.4 us (20%)
  waiting for transfers between devices  10.1 us (10%)
  between operations  1.5 us (1%)
    pallas_call x2, Pallas kernels, lateral(): pl.pallas_call(lateral_kernel, in_specs=[SMEM, HBM, HBM, HBM, UNREAD], ou...  19.9 us
    ppermute x12, starting transfers between devices, in_square(): lax.ppermute(blocks[k], 'space', [(s, s ^ k) for s in range(8)])  16.6 us
    pallas_call x2, Pallas kernels, pointwise(): pl.pallas_call(functools.partial(pointwise_kernel if keep else pointwise_...  12.8 us
    pallas_call x1, Pallas kernels, finish(): pl.pallas_call(finish_kernel, in_specs=[SMEM] + [VMEM] * 8 + [HBM, VMEM,...  12.3 us
    ppermute x12, waiting for transfers between devices, in_square(): lax.ppermute(blocks[k], 'space', [(s, s ^ k) for s in range(8)])  8.62 us
    pallas_call x1, Pallas kernels, pack_weight(): pl.pallas_call(pack_kernel, in_specs=[SMEM, HBM, VMEM, HBM, UNREAD], out_...  7.53 us
    pallas_call x1, Pallas kernels, weight_grad(): pl.pallas_call(weight_grad_kernel, grid=(4,), in_specs=[SMEM] + [VMEM] *...  7.09 us
    pallas_call x1, Pallas kernels, back_modes(): pl.pallas_call(back_modes_kernel, in_specs=[SMEM] + [VMEM] * 5 + [HBM, VM...  5.67 us
  transfers between devices with their start and end apart: 17, of which 5 were waited for; matrix products, arithmetic and copies ran while one was open for 0% of the time, Pallas kernels for 50%

profile of v1, /device:TPU:0, one launch (start us, length us, event | category | flops | bytes accessed | tf_op | source)
XLA Modules:
  0.0 104.1 jit_solution(15103604939454490436)
XLA Ops:
  0.6 0.0 copy-start
  0.6 10.0 %cotangent_lateral.1 = (bf16[2,16,4096]{2,1,0:T(8,128)(2,1)S(1)}, bf16[2,16,4096]{2,1,0:T(8,128)(2,1)S(1)}, bf16[2,16,4096]{2,1,0:T(8,128)(2,1)S(1)}, bf16[2,16,4096]{2,1,0:T(8,128)(2,1)S(1)}) custom-call(s32[1]{0:T(128)} %bitcast.me_ref._, bf16[16,32,128,128]{3,2,1,0:T(8,128)(2,1)} %bitcast.8, bf16[1024,256]{1,0:T(8,128)(2,1)} %constant.18.clone.z_hbm, ...), custom_call_target="tpu_custom_call" | custom-call | flops 60000000 | bytes 1024 | tf_op jit(solution)/shard_map/cotangent_lateral/pallas_call | solution.py:277
  10.6 3.0 %collective-permute-start = (bf16[2,16,4096]{2,1,0:T(8,128)(2,1)S(1)}, bf16[2,16,4096]{2,1,0:T(8,128)(2,1)S(1)}, u32[]{:S(2)}, u32[]{:S(2)}) collective-permute-start(bf16[2,16,4096]{2,1,0:T(8,128)(2,1)S(1)} %get-tuple-element.32), channel_id=1, source_target_pairs={{0,2},{2,0},{4,6},{6,4},{8,10},{10,8},{12,14},{14,12},{1,3},{3,1},... | collective-permute-start | bytes 786440 | tf_op jit(solution)/shard_map/ppermute | solution.py:876
  13.6 1.6 %collective-permute-start.1 = (bf16[2,16,4096]{2,1,0:T(8,128)(2,1)S(1)}, bf16[2,16,4096]{2,1,0:T(8,128)(2,1)S(1)}, u32[]{:S(2)}, u32[]{:S(2)}) collective-permute-start(bf16[2,16,4096]{2,1,0:T(8,128)(2,1)S(1)} %get-tuple-element.33), channel_id=1, source_target_pairs={{0,4},{2,6},{4,0},{6,2},{8,12},{10,14},{12,8},{14,10},{1,5},{3,7},... | collective-permute-start | bytes 786440 | tf_op jit(solution)/shard_map/ppermute | solution.py:876
  15.2 0.0 collective-permute-start.2
  15.2 10.0 %volume_lateral.1 = (bf16[2,16,4096]{2,1,0:T(8,128)(2,1)S(1)}, bf16[2,16,4096]{2,1,0:T(8,128)(2,1)S(1)}, bf16[2,16,4096]{2,1,0:T(8,128)(2,1)S(1)}, bf16[2,16,4096]{2,1,0:T(8,128)(2,1)S(1)}) custom-call(s32[1]{0:T(128)} %bitcast.me_ref._, bf16[16,32,128,128]{3,2,1,0:T(8,128)(2,1)} %bitcast.12, bf16[1024,256]{1,0:T(8,128)(2,1)} %constant.18.clone.z_hbm, ...), custom_call_target="tpu_custom_call" | custom-call | flops 60000000 | bytes 1024 | tf_op jit(solution)/shard_map/volume_lateral/pallas_call | solution.py:277
  25.2 0.0 collective-permute-done.r1
  25.2 0.0 collective-permute-done.1.r2
  25.2 1.6 %collective-permute-done.2.r3 = bf16[2,16,4096]{2,1,0:T(8,128)(2,1)S(1)} collective-permute-done((bf16[2,16,4096]{2,1,0:T(8,128)(2,1)S(1)}, bf16[2,16,4096]{2,1,0:T(8,128)(2,1)S(1)}, u32[]{:S(2)}, u32[]{:S(2)}) %collective-permute-start.2) | collective-permute-done | bytes 262176 | tf_op jit(solution)/shard_map/ppermute | solution.py:876
  26.8 0.9 cotangent_partner.1
  27.8 2.8 %collective-permute-start.3 = (bf16[64,2048]{1,0:T(8,128)(2,1)S(1)}, bf16[64,2048]{1,0:T(8,128)(2,1)S(1)}, u32[]{:S(2)}, u32[]{:S(2)}) collective-permute-start(bf16[64,2048]{1,0:T(8,128)(2,1)S(1)} %get-tuple-element.36._), channel_id=1, source_target_pairs={{0,8},{2,10},{4,12},{6,14},{8,0},{10,2},{12,4},{14,6},{1,9},{3,11}... | collective-permute-start | bytes 786440 | tf_op jit(solution)/shard_map/ppermute | solution.py:895
  30.6 1.6 %collective-permute-start.5 = (bf16[2,16,4096]{2,1,0:T(8,128)(2,1)S(1)}, bf16[2,16,4096]{2,1,0:T(8,128)(2,1)S(1)}, u32[]{:S(2)}, u32[]{:S(2)}) collective-permute-start(bf16[2,16,4096]{2,1,0:T(8,128)(2,1)S(1)} %get-tuple-element.42), channel_id=1, source_target_pairs={{0,4},{2,6},{4,0},{6,2},{8,12},{10,14},{12,8},{14,10},{1,5},{3,7},... | collective-permute-start | bytes 786440 | tf_op jit(solution)/shard_map/ppermute | solution.py:876
  32.2 1.4 %collective-permute-start.6 = (bf16[2,16,4096]{2,1,0:T(8,128)(2,1)S(1)}, bf16[2,16,4096]{2,1,0:T(8,128)(2,1)S(1)}, u32[]{:S(2)}, u32[]{:S(2)}) collective-permute-start(bf16[2,16,4096]{2,1,0:T(8,128)(2,1)S(1)} %get-tuple-element.43), channel_id=1, source_target_pairs={{0,6},{2,4},{4,2},{6,0},{8,14},{10,12},{12,10},{14,8},{1,7},{3,5},... | collective-permute-start | bytes 786440 | tf_op jit(solution)/shard_map/ppermute | solution.py:876
  33.5 0.5 collective-permute-start.4
  34.7 0.0 copy-done
  34.7 7.5 %pack_weight.1 = (bf16[2,16,32,32,128]{4,3,2,1,0:T(8,128)(2,1)S(1)}, bf16[256,256]{1,0:T(8,128)(2,1)}) custom-call(s32[1]{0:T(128)S(6)} %copy.25.at_ref, bf16[2,32,32,32,64]{4,3,2,1,0:T(8,128)(2,1)} %bitcast.14, bf16[32,32]{1,0:T(8,128)(2,1)S(1)} %copy-done, bf16[32,4096]{1,0:T(8,128)(2,1)} %bitcast.15, bf16[64,2048]{1,0:T(8,128)(2,1)S(1)} %get-tuple-element.36._), custom_call_target="tpu_custom_call" | custom-call | flops 48000000 | bytes 1024 | tf_op jit(solution)/shard_map/pack_weight/pallas_call | solution.py:454
  42.3 0.0 collective-permute-done.3.other_ref
  42.3 5.7 %back_modes.1 = (bf16[32,32,128]{2,1,0:T(8,128)(2,1)S(1)}, bf16[64,2048]{1,0:T(8,128)(2,1)S(1)}) custom-call(s32[1]{0:T(128)} %bitcast.me_ref._, bf16[2,16,4096]{2,1,0:T(8,128)(2,1)S(1)} %get-tuple-element.31._.r0, bf16[2,16,4096]{2,1,0:T(8,128)(2,1)S(1)} %collective-permute-done.r1, bf16[2,16,4096]{2,1,0:T(8,128)(2,1)S(1)} %collective-permute-done.1.r2, ...), custom_call_target="tpu_custom_call" | custom-call | flops 36000000 | bytes 1024 | tf_op jit(solution)/shard_map/back_modes/pallas_call | solution.py:536
  48.0 0.2 collective-permute-start.10
  48.2 0.0 collective-permute-done.5.r2
  48.2 0.0 collective-permute-done.6.r3
  48.2 0.0 collective-permute-done.4.r1
  48.3 1.0 volume_partner.1
  49.2 1.1 %own_planes.1 = (bf16[64,2048]{1,0:T(8,128)(2,1)S(1)}, bf16[16,4096]{1,0:T(8,128)(2,1)S(1)}, bf16[16,4096]{1,0:T(8,128)(2,1)S(1)}, bf16[16,4096]{1,0:T(8,128)(2,1)S(1)}, bf16[16,4096]{1,0:T(8,128)(2,1)S(1)}) custom-call(s32[1]{0:T(128)} %bitcast.me_ref._, bf16[64,2048]{1,0:T(8,128)(2,1)S(1)} %get-tuple-element.39.b_ref, ...), custom_call_target="tpu_custom_call", output_to_operand_aliasing={{0}: (3, {})} | custom-call | flops 6000000 | bytes 1024 | tf_op jit(solution)/shard_map/own_planes/pallas_call | solution.py:574
  50.3 1.7 %collective-permute-start.7 = (bf16[16,4096]{1,0:T(8,128)(2,1)S(1)}, bf16[16,4096]{1,0:T(8,128)(2,1)S(1)}, u32[]{:S(2)}, u32[]{:S(2)}) collective-permute-start(bf16[16,4096]{1,0:T(8,128)(2,1)S(1)} %get-tuple-element.47), channel_id=1, source_target_pairs={{0,2},{2,0},{4,6},{6,4},{8,10},{10,8},{12,14},{14,12},{1,3},{3,1},... | collective-permute-start | bytes 393224 | tf_op jit(solution)/shard_map/ppermute | solution.py:876
  52.0 2.9 %collective-permute-start.8 = (bf16[16,4096]{1,0:T(8,128)(2,1)S(1)}, bf16[16,4096]{1,0:T(8,128)(2,1)S(1)}, u32[]{:S(2)}, u32[]{:S(2)}) collective-permute-start(bf16[16,4096]{1,0:T(8,128)(2,1)S(1)} %get-tuple-element.48), channel_id=1, source_target_pairs={{0,4},{2,6},{4,0},{6,2},{8,12},{10,14},{12,8},{14,10},{1,5},{3,7},... | collective-permute-start | bytes 393224 | tf_op jit(solution)/shard_map/ppermute | solution.py:876
  54.9 0.0 collective-permute-start.9
  54.9 7.6 %pointwise_first.1 = (bf16[8,32,128,128]{3,2,1,0:T(8,128)(2,1)}, bf16[16,4096]{1,0:T(8,128)(2,1)S(1)}) custom-call(bf16[16,32,128,128]{3,2,1,0:T(8,128)(2,1)} %bitcast.9, bf16[256,256]{1,0:T(8,128)(2,1)} %get-tuple-element.37.k_hbm, bf16[16,4096]{1,0:T(8,128)(2,1)S(1)} %get-tuple-element.45._), custom_call_target="tpu_custom_call", output_to_operand_aliasing={{1}: (2, {})} | custom-call | flops 30000000 | bytes 1024 | tf_op jit(solution)/shard_map/pointwise_first/pallas_call | solution.py:737
  62.5 0.0 collective-permute-done.7.rest_1_.n1
  62.6 0.0 collective-permute-done.8.rest_2_.n2
  62.6 1.8 %collective-permute-done.9.rest_3_.n3 = bf16[16,4096]{1,0:T(8,128)(2,1)S(1)} collective-permute-done((bf16[16,4096]{1,0:T(8,128)(2,1)S(1)}, bf16[16,4096]{1,0:T(8,128)(2,1)S(1)}, u32[]{:S(2)}, u32[]{:S(2)}) %collective-permute-start.9) | collective-permute-done | bytes 131104 | tf_op jit(solution)/shard_map/ppermute | solution.py:876
  64.3 0.0 collective-permute-done.10.b_ref
  64.4 1.1 %partner_planes.1 = (bf16[64,2048]{1,0:T(8,128)(2,1)S(1)}, bf16[16,4096]{1,0:T(8,128)(2,1)S(1)}, bf16[16,4096]{1,0:T(8,128)(2,1)S(1)}, bf16[16,4096]{1,0:T(8,128)(2,1)S(1)}, bf16[16,4096]{1,0:T(8,128)(2,1)S(1)}) custom-call(s32[1]{0:T(128)} %bitcast.me_ref._, bf16[64,2048]{1,0:T(8,128)(2,1)S(1)} %collective-permute-done.10.b_ref, ...), custom_call_target="tpu_custom_call", output_to_operand_aliasing={{0}: (3, {})} | custom-call | flops 6000000 | bytes 1024 | tf_op jit(solution)/shard_map/partner_planes/pallas_call | solution.py:574
  65.4 1.6 %collective-permute-start.14 = (bf16[64,2048]{1,0:T(8,128)(2,1)S(1)}, bf16[64,2048]{1,0:T(8,128)(2,1)S(1)}, u32[]{:S(2)}, u32[]{:S(2)}) collective-permute-start(bf16[64,2048]{1,0:T(8,128)(2,1)S(1)} %get-tuple-element.58), channel_id=1, source_target_pairs={{0,8},{2,10},{4,12},{6,14},{8,0},{10,2},{12,4},{14,6},{1,9},{3,11}... | collective-permute-start | bytes 786440 | tf_op jit(solution)/shard_map/ppermute | solution.py:913
  67.0 0.5 collective-permute-start.11
  67.6 3.4 %collective-permute-start.12 = (bf16[16,4096]{1,0:T(8,128)(2,1)S(1)}, bf16[16,4096]{1,0:T(8,128)(2,1)S(1)}, u32[]{:S(2)}, u32[]{:S(2)}) collective-permute-start(bf16[16,4096]{1,0:T(8,128)(2,1)S(1)} %get-tuple-element.55), channel_id=1, source_target_pairs={{0,4},{2,6},{4,0},{6,2},{8,12},{10,14},{12,8},{14,10},{1,5},{3,7},... | collective-permute-start | bytes 393224 | tf_op jit(solution)/shard_map/ppermute | solution.py:876
  71.0 0.0 collective-permute-start.13
  71.0 0.0 collective-permute-start.16
  71.0 5.2 %pointwise_second.1 = (bf16[8,32,128,128]{3,2,1,0:T(8,128)(2,1)S(1)}, bf16[16,4096]{1,0:T(8,128)(2,1)S(1)}) custom-call(bf16[16,32,128,128]{3,2,1,0:T(8,128)(2,1)} %bitcast.10, bf16[256,256]{1,0:T(8,128)(2,1)} %get-tuple-element.37.k_hbm, bf16[16,4096]{1,0:T(8,128)(2,1)S(1)} %get-tuple-element.52._), custom_call_target="tpu_custom_call", output_to_operand_aliasing={{1}: (2, {})} | custom-call | flops 30000000 | bytes 1024 | tf_op jit(solution)/shard_map/pointwise_second/pallas_call | solution.py:737
  76.2 0.0 collective-permute-done.11.f1
  76.2 3.9 %collective-permute-done.12.f2 = bf16[16,4096]{1,0:T(8,128)(2,1)S(1)} collective-permute-done((bf16[16,4096]{1,0:T(8,128)(2,1)S(1)}, bf16[16,4096]{1,0:T(8,128)(2,1)S(1)}, u32[]{:S(2)}, u32[]{:S(2)}) %collective-permute-start.12) | collective-permute-done | bytes 131104 | tf_op jit(solution)/shard_map/ppermute | solution.py:876
  80.1 1.3 %collective-permute-done.13.f3 = bf16[16,4096]{1,0:T(8,128)(2,1)S(1)} collective-permute-done((bf16[16,4096]{1,0:T(8,128)(2,1)S(1)}, bf16[16,4096]{1,0:T(8,128)(2,1)S(1)}, u32[]{:S(2)}, u32[]{:S(2)}) %collective-permute-start.13) | collective-permute-done | bytes 131104 | tf_op jit(solution)/shard_map/ppermute | solution.py:876
  81.4 12.3 %finish.1.rest_0_ = bf16[16,32,128,128]{3,2,1,0:T(8,128)(2,1)} custom-call(s32[1]{0:T(128)} %bitcast.me_ref._, bf16[16,4096]{1,0:T(8,128)(2,1)S(1)} %get-tuple-element.46.n0, bf16[16,4096]{1,0:T(8,128)(2,1)S(1)} %collective-permute-done.7.rest_1_.n1, bf16[16,4096]{1,0:T(8,128)(2,1)S(1)} %collective-permute-done.8.rest_2_.n2, ...), custom_call_target="tpu_custom_call" | custom-call | flops 72000000 | bytes 1024 | tf_op jit(solution)/shard_map/finish/pallas_call | solution.py:846
  93.7 0.0 collective-permute-done.14.other_ref
  93.7 1.7 %volume_modes.1.u0_ref = bf16[32,32,128]{2,1,0:T(8,128)(2,1)S(1)} custom-call(s32[1]{0:T(128)} %bitcast.me_ref._, bf16[2,16,4096]{2,1,0:T(8,128)(2,1)S(1)} %get-tuple-element.40.r0, bf16[2,16,4096]{2,1,0:T(8,128)(2,1)S(1)} %collective-permute-done.4.r1, bf16[2,16,4096]{2,1,0:T(8,128)(2,1)S(1)} %collective-permute-done.5.r2, ...), custom_call_target="tpu_custom_call" | custom-call | flops 9000000 | bytes 1024 | tf_op jit(solution)/shard_map/volume_modes/pallas_call | solution.py:386
  95.4 0.1 collective-permute-start.15
  95.5 0.0 collective-permute-done.16.g1_ref
  95.5 1.5 %collective-permute-done.15.u1_ref = bf16[32,32,128]{2,1,0:T(8,128)(2,1)S(1)} collective-permute-done((bf16[32,32,128]{2,1,0:T(8,128)(2,1)S(1)}, bf16[32,32,128]{2,1,0:T(8,128)(2,1)S(1)}, u32[]{:S(2)}, u32[]{:S(2)}) %collective-permute-start.15) | collective-permute-done | bytes 262176 | tf_op jit(solution)/shard_map/ppermute | solution.py:917
  97.0 7.1 %weight_grad.1 = f32[2,32,32,16,64]{4,3,2,1,0:T(8,128)} custom-call(s32[1]{0:T(128)} %bitcast.6.half_ref, bf16[32,32,128]{2,1,0:T(8,128)(2,1)S(1)} %volume_modes.1.u0_ref, bf16[32,32,128]{2,1,0:T(8,128)(2,1)S(1)} %collective-permute-done.15.u1_ref, bf16[32,32,128]{2,1,0:T(8,128)(2,1)S(1)} %get-tuple-element.59.g0_ref, ...), custom_call_target="tpu_custom_call" | custom-call | flops 48000000 | bytes 1024 | tf_op jit(solution)/shard_map/weight_grad/pallas_call | solution.py:624
  (1 shorter events, 0.0 us)
Async XLA Ops:
  0.6 34.1 %copy-start = (bf16[32,32]{1,0:T(8,128)(2,1)S(1)}, bf16[32,32]{1,0:T(8,128)(2,1)}, u32[]{:S(2)}) copy-start(bf16[32,32]{1,0:T(8,128)(2,1)} %p_ref.1) | copy-start | bytes 6148
  10.6 14.6 %collective-permute-start = (bf16[2,16,4096]{2,1,0:T(8,128)(2,1)S(1)}, bf16[2,16,4096]{2,1,0:T(8,128)(2,1)S(1)}, u32[]{:S(2)}, u32[]{:S(2)}) collective-permute-start(bf16[2,16,4096]{2,1,0:T(8,128)(2,1)S(1)} %get-tuple-element.32), channel_id=1, source_target_pairs={{0,2},{2,0},{4,6},{6,4},{8,10},{10,8},{12,14},{14,12},{1,3},{3,1},... | collective-permute-start | bytes 786440 | tf_op jit(solution)/shard_map/ppermute | solution.py:876
  13.6 11.6 %collective-permute-start.1 = (bf16[2,16,4096]{2,1,0:T(8,128)(2,1)S(1)}, bf16[2,16,4096]{2,1,0:T(8,128)(2,1)S(1)}, u32[]{:S(2)}, u32[]{:S(2)}) collective-permute-start(bf16[2,16,4096]{2,1,0:T(8,128)(2,1)S(1)} %get-tuple-element.33), channel_id=1, source_target_pairs={{0,4},{2,6},{4,0},{6,2},{8,12},{10,14},{12,8},{14,10},{1,5},{3,7},... | collective-permute-start | bytes 786440 | tf_op jit(solution)/shard_map/ppermute | solution.py:876
  15.2 11.6 %collective-permute-start.2 = (bf16[2,16,4096]{2,1,0:T(8,128)(2,1)S(1)}, bf16[2,16,4096]{2,1,0:T(8,128)(2,1)S(1)}, u32[]{:S(2)}, u32[]{:S(2)}) collective-permute-start(bf16[2,16,4096]{2,1,0:T(8,128)(2,1)S(1)} %get-tuple-element.34), channel_id=1, source_target_pairs={{0,6},{2,4},{4,2},{6,0},{8,14},{10,12},{12,10},{14,8},{1,7},{3,5},... | collective-permute-start | bytes 786440 | tf_op jit(solution)/shard_map/ppermute | solution.py:876
  27.8 14.5 %collective-permute-start.3 = (bf16[64,2048]{1,0:T(8,128)(2,1)S(1)}, bf16[64,2048]{1,0:T(8,128)(2,1)S(1)}, u32[]{:S(2)}, u32[]{:S(2)}) collective-permute-start(bf16[64,2048]{1,0:T(8,128)(2,1)S(1)} %get-tuple-element.36._), channel_id=1, source_target_pairs={{0,8},{2,10},{4,12},{6,14},{8,0},{10,2},{12,4},{14,6},{1,9},{3,11}... | collective-permute-start | bytes 786440 | tf_op jit(solution)/shard_map/ppermute | solution.py:895
  30.6 17.6 %collective-permute-start.5 = (bf16[2,16,4096]{2,1,0:T(8,128)(2,1)S(1)}, bf16[2,16,4096]{2,1,0:T(8,128)(2,1)S(1)}, u32[]{:S(2)}, u32[]{:S(2)}) collective-permute-start(bf16[2,16,4096]{2,1,0:T(8,128)(2,1)S(1)} %get-tuple-element.42), channel_id=1, source_target_pairs={{0,4},{2,6},{4,0},{6,2},{8,12},{10,14},{12,8},{14,10},{1,5},{3,7},... | collective-permute-start | bytes 786440 | tf_op jit(solution)/shard_map/ppermute | solution.py:876
  32.2 16.1 %collective-permute-start.6 = (bf16[2,16,4096]{2,1,0:T(8,128)(2,1)S(1)}, bf16[2,16,4096]{2,1,0:T(8,128)(2,1)S(1)}, u32[]{:S(2)}, u32[]{:S(2)}) collective-permute-start(bf16[2,16,4096]{2,1,0:T(8,128)(2,1)S(1)} %get-tuple-element.43), channel_id=1, source_target_pairs={{0,6},{2,4},{4,2},{6,0},{8,14},{10,12},{12,10},{14,8},{1,7},{3,5},... | collective-permute-start | bytes 786440 | tf_op jit(solution)/shard_map/ppermute | solution.py:876
  33.5 14.7 %collective-permute-start.4 = (bf16[2,16,4096]{2,1,0:T(8,128)(2,1)S(1)}, bf16[2,16,4096]{2,1,0:T(8,128)(2,1)S(1)}, u32[]{:S(2)}, u32[]{:S(2)}) collective-permute-start(bf16[2,16,4096]{2,1,0:T(8,128)(2,1)S(1)} %get-tuple-element.41), channel_id=1, source_target_pairs={{0,2},{2,0},{4,6},{6,4},{8,10},{10,8},{12,14},{14,12},{1,3},{3,1},... | collective-permute-start | bytes 786440 | tf_op jit(solution)/shard_map/ppermute | solution.py:876
  48.0 16.4 %collective-permute-start.10 = (bf16[64,2048]{1,0:T(8,128)(2,1)S(1)}, bf16[64,2048]{1,0:T(8,128)(2,1)S(1)}, u32[]{:S(2)}, u32[]{:S(2)}) collective-permute-start(bf16[64,2048]{1,0:T(8,128)(2,1)S(1)} %get-tuple-element.39.b_ref), channel_id=1, source_target_pairs={{0,8},{2,10},{4,12},{6,14},{8,0},{10,2},{12,4},{14,6},{1,9},{3,11}... | collective-permute-start | bytes 786440 | tf_op jit(solution)/shard_map/ppermute | solution.py:899
  50.3 12.2 %collective-permute-start.7 = (bf16[16,4096]{1,0:T(8,128)(2,1)S(1)}, bf16[16,4096]{1,0:T(8,128)(2,1)S(1)}, u32[]{:S(2)}, u32[]{:S(2)}) collective-permute-start(bf16[16,4096]{1,0:T(8,128)(2,1)S(1)} %get-tuple-element.47), channel_id=1, source_target_pairs={{0,2},{2,0},{4,6},{6,4},{8,10},{10,8},{12,14},{14,12},{1,3},{3,1},... | collective-permute-start | bytes 393224 | tf_op jit(solution)/shard_map/ppermute | solution.py:876
  52.0 10.6 %collective-permute-start.8 = (bf16[16,4096]{1,0:T(8,128)(2,1)S(1)}, bf16[16,4096]{1,0:T(8,128)(2,1)S(1)}, u32[]{:S(2)}, u32[]{:S(2)}) collective-permute-start(bf16[16,4096]{1,0:T(8,128)(2,1)S(1)} %get-tuple-element.48), channel_id=1, source_target_pairs={{0,4},{2,6},{4,0},{6,2},{8,12},{10,14},{12,8},{14,10},{1,5},{3,7},... | collective-permute-start | bytes 393224 | tf_op jit(solution)/shard_map/ppermute | solution.py:876
  54.9 9.4 %collective-permute-start.9 = (bf16[16,4096]{1,0:T(8,128)(2,1)S(1)}, bf16[16,4096]{1,0:T(8,128)(2,1)S(1)}, u32[]{:S(2)}, u32[]{:S(2)}) collective-permute-start(bf16[16,4096]{1,0:T(8,128)(2,1)S(1)} %get-tuple-element.49), channel_id=1, source_target_pairs={{0,6},{2,4},{4,2},{6,0},{8,14},{10,12},{12,10},{14,8},{1,7},{3,5},... | collective-permute-start | bytes 393224 | tf_op jit(solution)/shard_map/ppermute | solution.py:876
  65.4 28.2 %collective-permute-start.14 = (bf16[64,2048]{1,0:T(8,128)(2,1)S(1)}, bf16[64,2048]{1,0:T(8,128)(2,1)S(1)}, u32[]{:S(2)}, u32[]{:S(2)}) collective-permute-start(bf16[64,2048]{1,0:T(8,128)(2,1)S(1)} %get-tuple-element.58), channel_id=1, source_target_pairs={{0,8},{2,10},{4,12},{6,14},{8,0},{10,2},{12,4},{14,6},{1,9},{3,11}... | collective-permute-start | bytes 786440 | tf_op jit(solution)/shard_map/ppermute | solution.py:913
  67.0 9.2 %collective-permute-start.11 = (bf16[16,4096]{1,0:T(8,128)(2,1)S(1)}, bf16[16,4096]{1,0:T(8,128)(2,1)S(1)}, u32[]{:S(2)}, u32[]{:S(2)}) collective-permute-start(bf16[16,4096]{1,0:T(8,128)(2,1)S(1)} %get-tuple-element.54), channel_id=1, source_target_pairs={{0,2},{2,0},{4,6},{6,4},{8,10},{10,8},{12,14},{14,12},{1,3},{3,1},... | collective-permute-start | bytes 393224 | tf_op jit(solution)/shard_map/ppermute | solution.py:876
  67.6 12.5 %collective-permute-start.12 = (bf16[16,4096]{1,0:T(8,128)(2,1)S(1)}, bf16[16,4096]{1,0:T(8,128)(2,1)S(1)}, u32[]{:S(2)}, u32[]{:S(2)}) collective-permute-start(bf16[16,4096]{1,0:T(8,128)(2,1)S(1)} %get-tuple-element.55), channel_id=1, source_target_pairs={{0,4},{2,6},{4,0},{6,2},{8,12},{10,14},{12,8},{14,10},{1,5},{3,7},... | collective-permute-start | bytes 393224 | tf_op jit(solution)/shard_map/ppermute | solution.py:876
  71.0 10.4 %collective-permute-start.13 = (bf16[16,4096]{1,0:T(8,128)(2,1)S(1)}, bf16[16,4096]{1,0:T(8,128)(2,1)S(1)}, u32[]{:S(2)}, u32[]{:S(2)}) collective-permute-start(bf16[16,4096]{1,0:T(8,128)(2,1)S(1)} %get-tuple-element.56), channel_id=1, source_target_pairs={{0,6},{2,4},{4,2},{6,0},{8,14},{10,12},{12,10},{14,8},{1,7},{3,5},... | collective-permute-start | bytes 393224 | tf_op jit(solution)/shard_map/ppermute | solution.py:876
  71.0 24.5 %collective-permute-start.16 = (bf16[32,32,128]{2,1,0:T(8,128)(2,1)S(1)}, bf16[32,32,128]{2,1,0:T(8,128)(2,1)S(1)}, u32[]{:S(2)}, u32[]{:S(2)}) collective-permute-start(bf16[32,32,128]{2,1,0:T(8,128)(2,1)S(1)} %get-tuple-element.59.g0_ref), channel_id=1, source_target_pairs={{0,1},{1,0},{2,3},{3,2},{4,5},{5,4},{6,7},{7,6},{8,9},{9,8},{10,11... | collective-permute-start | bytes 786440 | tf_op jit(solution)/shard_map/ppermute | solution.py:916
  95.4 1.6 %collective-permute-start.15 = (bf16[32,32,128]{2,1,0:T(8,128)(2,1)S(1)}, bf16[32,32,128]{2,1,0:T(8,128)(2,1)S(1)}, u32[]{:S(2)}, u32[]{:S(2)}) collective-permute-start(bf16[32,32,128]{2,1,0:T(8,128)(2,1)S(1)} %volume_modes.1.u0_ref), channel_id=1, source_target_pairs={{0,1},{1,0},{2,3},{3,2},{4,5},{5,4},{6,7},{7,6},{8,9},{9,8},{10,11... | collective-permute-start | bytes 786440 | tf_op jit(solution)/shard_map/ppermute | solution.py:917

commit v2 on v1

--- a/solution.py
+++ b/solution.py
@@ -788,54 +788,62 @@
     for x in range(i_ref.shape[0]):
         load(x).start()
 
-    def step(t, point):
-        @pl.when(t >= slots)
-        def _():
-            save(t - slots).wait()
-
-        x = place(t)
-        slot = lax.rem(t, slots)
-        planes = jnp.concatenate(
-            [s_ref[n, pl.ds(x, 64, stride=16), :].astype(BF) for n in range(4)], axis=1
-        )
-        rows = dot(y_ref[...], planes).astype(BF)
-        lhs = jnp.concatenate(
-            [
+    def pair(t, points):
+        for k in range(2):
+
+            @pl.when(t + k >= slots)
+            def _():
+                save(t + k - slots).wait()
+
+        sides = []
+        for k in range(2):
+            x = place(t + k)
+            planes = jnp.concatenate(
+                [s_ref[n, pl.ds(x, 64, stride=16), :].astype(BF) for n in range(4)], axis=1
+            )
+            rows = dot(y_ref[...], planes).astype(BF)
+            sides += [
                 jnp.concatenate(
                     [rows[:128, co * 128 : co * 128 + 128], rows[128:, co * 128 : co * 128 + 128]],
                     axis=1,
                 )
                 for co in range(4)
-            ],
-            axis=0,
-        )
+            ]
+        lhs = jnp.concatenate(sides, axis=0)
         for n in range(4):
             part = dot(lhs, z_ref[:, n * 256 : n * 256 + 256])
-            for co in range(4):
-                for j in range(2):
-                    c = co * 8 + n * 2 + j
-                    b_ref[slot, c] = (
-                        part[co * 128 : co * 128 + 128, j * 128 : j * 128 + 128]
-                        + point[c].astype(F32)
-                    ).astype(BF)
-        save(t).start()
-
-    def kept(t, carry):
-        step(t, q_ref.at[t])
+            for k in range(2):
+                slot = lax.rem(t + k, slots)
+                for co in range(4):
+                    for j in range(2):
+                        c = co * 8 + n * 2 + j
+                        row = (k * 4 + co) * 128
+                        b_ref[slot, c] = (
+                            part[row : row + 128, j * 128 : j * 128 + 128]
+                            + points[k][c].astype(F32)
+                        ).astype(BF)
+        for k in range(2):
+            save(t + k).start()
+
+    def kept(i, carry):
+        pair(2 * i, [q_ref.at[2 * i + k] for k in range(2)])
         return carry
 
-    def loaded(x, carry):
-        load(x).wait()
-        step(x + total - split, i_ref.at[lax.rem(x, i_ref.shape[0])])
-
-        @pl.when(x + i_ref.shape[0] < split)
-        def _():
-            load(x + i_ref.shape[0]).start()
+    def loaded(i, carry):
+        ring = i_ref.shape[0]
+        for k in range(2):
+            load(2 * i + k).wait()
+        pair(2 * i + total - split, [i_ref.at[lax.rem(2 * i + k, ring)] for k in range(2)])
+        for k in range(2):
+
+            @pl.when(2 * i + k + ring < split)
+            def _():
+                load(2 * i + k + ring).start()
 
         return carry
 
-    lax.fori_loop(0, total - split, kept, 0)
-    lax.fori_loop(0, split, loaded, 0)
+    lax.fori_loop(0, (total - split) // 2, kept, 0)
+    lax.fori_loop(0, split // 2, loaded, 0)
     for t in range(total - slots, total):
         save(t).wait()
 

time: 105 us -> 105 us (level)
  no operation moved by 1% of the time
where the time goes in v2:
time: 105 us; the launch traced here: 104 us
  Pallas kernels  71.4 us (68%)
  starting transfers between devices  21.4 us (20%)
  waiting for transfers between devices  10.1 us (10%)
  between operations  1.5 us (1%)
    pallas_call x2, Pallas kernels, lateral(): pl.pallas_call(lateral_kernel, in_specs=[SMEM, HBM, HBM, HBM, UNREAD], ou...  19.9 us
    ppermute x12, starting transfers between devices, in_square(): lax.ppermute(blocks[k], 'space', [(s, s ^ k) for s in range(8)])  16.6 us
    pallas_call x2, Pallas kernels, pointwise(): pl.pallas_call(functools.partial(pointwise_kernel if keep else pointwise_...  12.8 us
    pallas_call x1, Pallas kernels, finish(): pl.pallas_call(finish_kernel, in_specs=[SMEM] + [VMEM] * 8 + [HBM, VMEM,...  12.6 us
    ppermute x12, waiting for transfers between devices, in_square(): lax.ppermute(blocks[k], 'space', [(s, s ^ k) for s in range(8)])  8.62 us
    pallas_call x1, Pallas kernels, pack_weight(): pl.pallas_call(pack_kernel, in_specs=[SMEM, HBM, VMEM, HBM, UNREAD], out_...  7.53 us
    pallas_call x1, Pallas kernels, weight_grad(): pl.pallas_call(weight_grad_kernel, grid=(4,), in_specs=[SMEM] + [VMEM] *...  7.09 us
    pallas_call x1, Pallas kernels, back_modes(): pl.pallas_call(back_modes_kernel, in_specs=[SMEM] + [VMEM] * 5 + [HBM, VM...  5.67 us
  transfers between devices with their start and end apart: 17, of which 5 were waited for; matrix products, arithmetic and copies ran while one was open for 0% of the time, Pallas kernels for 50%

profile of v2, /device:TPU:0, one launch (start us, length us, event | category | flops | bytes accessed | tf_op | source)
XLA Modules:
  0.0 104.4 jit_solution(16103571665988540930)
XLA Ops:
  0.6 0.0 copy-start
  0.6 10.0 %cotangent_lateral.1 = (bf16[2,16,4096]{2,1,0:T(8,128)(2,1)S(1)}, bf16[2,16,4096]{2,1,0:T(8,128)(2,1)S(1)}, bf16[2,16,4096]{2,1,0:T(8,128)(2,1)S(1)}, bf16[2,16,4096]{2,1,0:T(8,128)(2,1)S(1)}) custom-call(s32[1]{0:T(128)} %bitcast.me_ref._, bf16[16,32,128,128]{3,2,1,0:T(8,128)(2,1)} %bitcast.8, bf16[1024,256]{1,0:T(8,128)(2,1)} %constant.18.clone.z_hbm, ...), custom_call_target="tpu_custom_call" | custom-call | flops 60000000 | bytes 1024 | tf_op jit(solution)/shard_map/cotangent_lateral/pallas_call | solution.py:277
  10.6 3.0 %collective-permute-start = (bf16[2,16,4096]{2,1,0:T(8,128)(2,1)S(1)}, bf16[2,16,4096]{2,1,0:T(8,128)(2,1)S(1)}, u32[]{:S(2)}, u32[]{:S(2)}) collective-permute-start(bf16[2,16,4096]{2,1,0:T(8,128)(2,1)S(1)} %get-tuple-element.32), channel_id=1, source_target_pairs={{0,2},{2,0},{4,6},{6,4},{8,10},{10,8},{12,14},{14,12},{1,3},{3,1},... | collective-permute-start | bytes 786440 | tf_op jit(solution)/shard_map/ppermute | solution.py:884
  13.6 1.6 %collective-permute-start.1 = (bf16[2,16,4096]{2,1,0:T(8,128)(2,1)S(1)}, bf16[2,16,4096]{2,1,0:T(8,128)(2,1)S(1)}, u32[]{:S(2)}, u32[]{:S(2)}) collective-permute-start(bf16[2,16,4096]{2,1,0:T(8,128)(2,1)S(1)} %get-tuple-element.33), channel_id=1, source_target_pairs={{0,4},{2,6},{4,0},{6,2},{8,12},{10,14},{12,8},{14,10},{1,5},{3,7},... | collective-permute-start | bytes 786440 | tf_op jit(solution)/shard_map/ppermute | solution.py:884
  15.2 0.0 collective-permute-start.2
  15.2 10.0 %volume_lateral.1 = (bf16[2,16,4096]{2,1,0:T(8,128)(2,1)S(1)}, bf16[2,16,4096]{2,1,0:T(8,128)(2,1)S(1)}, bf16[2,16,4096]{2,1,0:T(8,128)(2,1)S(1)}, bf16[2,16,4096]{2,1,0:T(8,128)(2,1)S(1)}) custom-call(s32[1]{0:T(128)} %bitcast.me_ref._, bf16[16,32,128,128]{3,2,1,0:T(8,128)(2,1)} %bitcast.12, bf16[1024,256]{1,0:T(8,128)(2,1)} %constant.18.clone.z_hbm, ...), custom_call_target="tpu_custom_call" | custom-call | flops 60000000 | bytes 1024 | tf_op jit(solution)/shard_map/volume_lateral/pallas_call | solution.py:277
  25.2 0.0 collective-permute-done.r1
  25.2 0.0 collective-permute-done.1.r2
  25.2 1.6 %collective-permute-done.2.r3 = bf16[2,16,4096]{2,1,0:T(8,128)(2,1)S(1)} collective-permute-done((bf16[2,16,4096]{2,1,0:T(8,128)(2,1)S(1)}, bf16[2,16,4096]{2,1,0:T(8,128)(2,1)S(1)}, u32[]{:S(2)}, u32[]{:S(2)}) %collective-permute-start.2) | collective-permute-done | bytes 262176 | tf_op jit(solution)/shard_map/ppermute | solution.py:884
  26.8 0.9 cotangent_partner.1
  27.8 2.8 %collective-permute-start.3 = (bf16[64,2048]{1,0:T(8,128)(2,1)S(1)}, bf16[64,2048]{1,0:T(8,128)(2,1)S(1)}, u32[]{:S(2)}, u32[]{:S(2)}) collective-permute-start(bf16[64,2048]{1,0:T(8,128)(2,1)S(1)} %get-tuple-element.36._), channel_id=1, source_target_pairs={{0,8},{2,10},{4,12},{6,14},{8,0},{10,2},{12,4},{14,6},{1,9},{3,11}... | collective-permute-start | bytes 786440 | tf_op jit(solution)/shard_map/ppermute | solution.py:903
  30.6 1.6 %collective-permute-start.5 = (bf16[2,16,4096]{2,1,0:T(8,128)(2,1)S(1)}, bf16[2,16,4096]{2,1,0:T(8,128)(2,1)S(1)}, u32[]{:S(2)}, u32[]{:S(2)}) collective-permute-start(bf16[2,16,4096]{2,1,0:T(8,128)(2,1)S(1)} %get-tuple-element.42), channel_id=1, source_target_pairs={{0,4},{2,6},{4,0},{6,2},{8,12},{10,14},{12,8},{14,10},{1,5},{3,7},... | collective-permute-start | bytes 786440 | tf_op jit(solution)/shard_map/ppermute | solution.py:884
  32.2 1.4 %collective-permute-start.6 = (bf16[2,16,4096]{2,1,0:T(8,128)(2,1)S(1)}, bf16[2,16,4096]{2,1,0:T(8,128)(2,1)S(1)}, u32[]{:S(2)}, u32[]{:S(2)}) collective-permute-start(bf16[2,16,4096]{2,1,0:T(8,128)(2,1)S(1)} %get-tuple-element.43), channel_id=1, source_target_pairs={{0,6},{2,4},{4,2},{6,0},{8,14},{10,12},{12,10},{14,8},{1,7},{3,5},... | collective-permute-start | bytes 786440 | tf_op jit(solution)/shard_map/ppermute | solution.py:884
  33.5 0.5 collective-permute-start.4
  34.7 0.0 copy-done
  34.7 7.5 %pack_weight.1 = (bf16[2,16,32,32,128]{4,3,2,1,0:T(8,128)(2,1)S(1)}, bf16[256,256]{1,0:T(8,128)(2,1)}) custom-call(s32[1]{0:T(128)S(6)} %copy.25.at_ref, bf16[2,32,32,32,64]{4,3,2,1,0:T(8,128)(2,1)} %bitcast.14, bf16[32,32]{1,0:T(8,128)(2,1)S(1)} %copy-done, bf16[32,4096]{1,0:T(8,128)(2,1)} %bitcast.15, bf16[64,2048]{1,0:T(8,128)(2,1)S(1)} %get-tuple-element.36._), custom_call_target="tpu_custom_call" | custom-call | flops 48000000 | bytes 1024 | tf_op jit(solution)/shard_map/pack_weight/pallas_call | solution.py:454
  42.3 0.0 collective-permute-done.3.other_ref
  42.3 5.7 %back_modes.1 = (bf16[32,32,128]{2,1,0:T(8,128)(2,1)S(1)}, bf16[64,2048]{1,0:T(8,128)(2,1)S(1)}) custom-call(s32[1]{0:T(128)} %bitcast.me_ref._, bf16[2,16,4096]{2,1,0:T(8,128)(2,1)S(1)} %get-tuple-element.31._.r0, bf16[2,16,4096]{2,1,0:T(8,128)(2,1)S(1)} %collective-permute-done.r1, bf16[2,16,4096]{2,1,0:T(8,128)(2,1)S(1)} %collective-permute-done.1.r2, ...), custom_call_target="tpu_custom_call" | custom-call | flops 36000000 | bytes 1024 | tf_op jit(solution)/shard_map/back_modes/pallas_call | solution.py:536
  48.0 0.2 collective-permute-start.10
  48.2 0.0 collective-permute-done.5.r2
  48.2 0.0 collective-permute-done.6.r3
  48.2 0.0 collective-permute-done.4.r1
  48.3 1.0 volume_partner.1
  49.2 1.1 %own_planes.1 = (bf16[64,2048]{1,0:T(8,128)(2,1)S(1)}, bf16[16,4096]{1,0:T(8,128)(2,1)S(1)}, bf16[16,4096]{1,0:T(8,128)(2,1)S(1)}, bf16[16,4096]{1,0:T(8,128)(2,1)S(1)}, bf16[16,4096]{1,0:T(8,128)(2,1)S(1)}) custom-call(s32[1]{0:T(128)} %bitcast.me_ref._, bf16[64,2048]{1,0:T(8,128)(2,1)S(1)} %get-tuple-element.39.b_ref, ...), custom_call_target="tpu_custom_call", output_to_operand_aliasing={{0}: (3, {})} | custom-call | flops 6000000 | bytes 1024 | tf_op jit(solution)/shard_map/own_planes/pallas_call | solution.py:574
  50.3 1.7 %collective-permute-start.7 = (bf16[16,4096]{1,0:T(8,128)(2,1)S(1)}, bf16[16,4096]{1,0:T(8,128)(2,1)S(1)}, u32[]{:S(2)}, u32[]{:S(2)}) collective-permute-start(bf16[16,4096]{1,0:T(8,128)(2,1)S(1)} %get-tuple-element.47), channel_id=1, source_target_pairs={{0,2},{2,0},{4,6},{6,4},{8,10},{10,8},{12,14},{14,12},{1,3},{3,1},... | collective-permute-start | bytes 393224 | tf_op jit(solution)/shard_map/ppermute | solution.py:884
  52.0 2.9 %collective-permute-start.8 = (bf16[16,4096]{1,0:T(8,128)(2,1)S(1)}, bf16[16,4096]{1,0:T(8,128)(2,1)S(1)}, u32[]{:S(2)}, u32[]{:S(2)}) collective-permute-start(bf16[16,4096]{1,0:T(8,128)(2,1)S(1)} %get-tuple-element.48), channel_id=1, source_target_pairs={{0,4},{2,6},{4,0},{6,2},{8,12},{10,14},{12,8},{14,10},{1,5},{3,7},... | collective-permute-start | bytes 393224 | tf_op jit(solution)/shard_map/ppermute | solution.py:884
  54.9 0.0 collective-permute-start.9
  54.9 7.6 %pointwise_first.1 = (bf16[8,32,128,128]{3,2,1,0:T(8,128)(2,1)}, bf16[16,4096]{1,0:T(8,128)(2,1)S(1)}) custom-call(bf16[16,32,128,128]{3,2,1,0:T(8,128)(2,1)} %bitcast.9, bf16[256,256]{1,0:T(8,128)(2,1)} %get-tuple-element.37.k_hbm, bf16[16,4096]{1,0:T(8,128)(2,1)S(1)} %get-tuple-element.45._), custom_call_target="tpu_custom_call", output_to_operand_aliasing={{1}: (2, {})} | custom-call | flops 30000000 | bytes 1024 | tf_op jit(solution)/shard_map/pointwise_first/pallas_call | solution.py:737
  62.5 0.0 collective-permute-done.7.rest_1_.n1
  62.6 0.0 collective-permute-done.8.rest_2_.n2
  62.6 1.8 %collective-permute-done.9.rest_3_.n3 = bf16[16,4096]{1,0:T(8,128)(2,1)S(1)} collective-permute-done((bf16[16,4096]{1,0:T(8,128)(2,1)S(1)}, bf16[16,4096]{1,0:T(8,128)(2,1)S(1)}, u32[]{:S(2)}, u32[]{:S(2)}) %collective-permute-start.9) | collective-permute-done | bytes 131104 | tf_op jit(solution)/shard_map/ppermute | solution.py:884
  64.3 0.0 collective-permute-done.10.b_ref
  64.4 1.1 %partner_planes.1 = (bf16[64,2048]{1,0:T(8,128)(2,1)S(1)}, bf16[16,4096]{1,0:T(8,128)(2,1)S(1)}, bf16[16,4096]{1,0:T(8,128)(2,1)S(1)}, bf16[16,4096]{1,0:T(8,128)(2,1)S(1)}, bf16[16,4096]{1,0:T(8,128)(2,1)S(1)}) custom-call(s32[1]{0:T(128)} %bitcast.me_ref._, bf16[64,2048]{1,0:T(8,128)(2,1)S(1)} %collective-permute-done.10.b_ref, ...), custom_call_target="tpu_custom_call", output_to_operand_aliasing={{0}: (3, {})} | custom-call | flops 6000000 | bytes 1024 | tf_op jit(solution)/shard_map/partner_planes/pallas_call | solution.py:574
  65.4 1.6 %collective-permute-start.14 = (bf16[64,2048]{1,0:T(8,128)(2,1)S(1)}, bf16[64,2048]{1,0:T(8,128)(2,1)S(1)}, u32[]{:S(2)}, u32[]{:S(2)}) collective-permute-start(bf16[64,2048]{1,0:T(8,128)(2,1)S(1)} %get-tuple-element.58), channel_id=1, source_target_pairs={{0,8},{2,10},{4,12},{6,14},{8,0},{10,2},{12,4},{14,6},{1,9},{3,11}... | collective-permute-start | bytes 786440 | tf_op jit(solution)/shard_map/ppermute | solution.py:921
  67.0 0.5 collective-permute-start.11
  67.6 3.4 %collective-permute-start.12 = (bf16[16,4096]{1,0:T(8,128)(2,1)S(1)}, bf16[16,4096]{1,0:T(8,128)(2,1)S(1)}, u32[]{:S(2)}, u32[]{:S(2)}) collective-permute-start(bf16[16,4096]{1,0:T(8,128)(2,1)S(1)} %get-tuple-element.55), channel_id=1, source_target_pairs={{0,4},{2,6},{4,0},{6,2},{8,12},{10,14},{12,8},{14,10},{1,5},{3,7},... | collective-permute-start | bytes 393224 | tf_op jit(solution)/shard_map/ppermute | solution.py:884
  71.0 0.0 collective-permute-start.13
  71.0 0.0 collective-permute-start.16
  71.0 5.2 %pointwise_second.1 = (bf16[8,32,128,128]{3,2,1,0:T(8,128)(2,1)S(1)}, bf16[16,4096]{1,0:T(8,128)(2,1)S(1)}) custom-call(bf16[16,32,128,128]{3,2,1,0:T(8,128)(2,1)} %bitcast.10, bf16[256,256]{1,0:T(8,128)(2,1)} %get-tuple-element.37.k_hbm, bf16[16,4096]{1,0:T(8,128)(2,1)S(1)} %get-tuple-element.52._), custom_call_target="tpu_custom_call", output_to_operand_aliasing={{1}: (2, {})} | custom-call | flops 30000000 | bytes 1024 | tf_op jit(solution)/shard_map/pointwise_second/pallas_call | solution.py:737
  76.2 0.0 collective-permute-done.11.f1
  76.2 3.9 %collective-permute-done.12.f2 = bf16[16,4096]{1,0:T(8,128)(2,1)S(1)} collective-permute-done((bf16[16,4096]{1,0:T(8,128)(2,1)S(1)}, bf16[16,4096]{1,0:T(8,128)(2,1)S(1)}, u32[]{:S(2)}, u32[]{:S(2)}) %collective-permute-start.12) | collective-permute-done | bytes 131104 | tf_op jit(solution)/shard_map/ppermute | solution.py:884
  80.1 1.3 %collective-permute-done.13.f3 = bf16[16,4096]{1,0:T(8,128)(2,1)S(1)} collective-permute-done((bf16[16,4096]{1,0:T(8,128)(2,1)S(1)}, bf16[16,4096]{1,0:T(8,128)(2,1)S(1)}, u32[]{:S(2)}, u32[]{:S(2)}) %collective-permute-start.13) | collective-permute-done | bytes 131104 | tf_op jit(solution)/shard_map/ppermute | solution.py:884
  81.4 12.6 %finish.1.rest_0_ = bf16[16,32,128,128]{3,2,1,0:T(8,128)(2,1)} custom-call(s32[1]{0:T(128)} %bitcast.me_ref._, bf16[16,4096]{1,0:T(8,128)(2,1)S(1)} %get-tuple-element.46.n0, bf16[16,4096]{1,0:T(8,128)(2,1)S(1)} %collective-permute-done.7.rest_1_.n1, bf16[16,4096]{1,0:T(8,128)(2,1)S(1)} %collective-permute-done.8.rest_2_.n2, ...), custom_call_target="tpu_custom_call" | custom-call | flops 72000000 | bytes 1024 | tf_op jit(solution)/shard_map/finish/pallas_call | solution.py:854
  94.0 0.0 collective-permute-done.14.other_ref
  94.0 1.7 %volume_modes.1.u0_ref = bf16[32,32,128]{2,1,0:T(8,128)(2,1)S(1)} custom-call(s32[1]{0:T(128)} %bitcast.me_ref._, bf16[2,16,4096]{2,1,0:T(8,128)(2,1)S(1)} %get-tuple-element.40.r0, bf16[2,16,4096]{2,1,0:T(8,128)(2,1)S(1)} %collective-permute-done.4.r1, bf16[2,16,4096]{2,1,0:T(8,128)(2,1)S(1)} %collective-permute-done.5.r2, ...), custom_call_target="tpu_custom_call" | custom-call | flops 9000000 | bytes 1024 | tf_op jit(solution)/shard_map/volume_modes/pallas_call | solution.py:386
  95.8 0.1 collective-permute-start.15
  95.8 0.0 collective-permute-done.16.g1_ref
  95.8 1.5 %collective-permute-done.15.u1_ref = bf16[32,32,128]{2,1,0:T(8,128)(2,1)S(1)} collective-permute-done((bf16[32,32,128]{2,1,0:T(8,128)(2,1)S(1)}, bf16[32,32,128]{2,1,0:T(8,128)(2,1)S(1)}, u32[]{:S(2)}, u32[]{:S(2)}) %collective-permute-start.15) | collective-permute-done | bytes 262176 | tf_op jit(solution)/shard_map/ppermute | solution.py:925
  97.4 7.1 %weight_grad.1 = f32[2,32,32,16,64]{4,3,2,1,0:T(8,128)} custom-call(s32[1]{0:T(128)} %bitcast.6.half_ref, bf16[32,32,128]{2,1,0:T(8,128)(2,1)S(1)} %volume_modes.1.u0_ref, bf16[32,32,128]{2,1,0:T(8,128)(2,1)S(1)} %collective-permute-done.15.u1_ref, bf16[32,32,128]{2,1,0:T(8,128)(2,1)S(1)} %get-tuple-element.59.g0_ref, ...), custom_call_target="tpu_custom_call" | custom-call | flops 48000000 | bytes 1024 | tf_op jit(solution)/shard_map/weight_grad/pallas_call | solution.py:624
  (1 shorter events, 0.0 us)
Async XLA Ops:
  0.6 34.1 %copy-start = (bf16[32,32]{1,0:T(8,128)(2,1)S(1)}, bf16[32,32]{1,0:T(8,128)(2,1)}, u32[]{:S(2)}) copy-start(bf16[32,32]{1,0:T(8,128)(2,1)} %p_ref.1) | copy-start | bytes 6148
  10.6 14.6 %collective-permute-start = (bf16[2,16,4096]{2,1,0:T(8,128)(2,1)S(1)}, bf16[2,16,4096]{2,1,0:T(8,128)(2,1)S(1)}, u32[]{:S(2)}, u32[]{:S(2)}) collective-permute-start(bf16[2,16,4096]{2,1,0:T(8,128)(2,1)S(1)} %get-tuple-element.32), channel_id=1, source_target_pairs={{0,2},{2,0},{4,6},{6,4},{8,10},{10,8},{12,14},{14,12},{1,3},{3,1},... | collective-permute-start | bytes 786440 | tf_op jit(solution)/shard_map/ppermute | solution.py:884
  13.6 11.6 %collective-permute-start.1 = (bf16[2,16,4096]{2,1,0:T(8,128)(2,1)S(1)}, bf16[2,16,4096]{2,1,0:T(8,128)(2,1)S(1)}, u32[]{:S(2)}, u32[]{:S(2)}) collective-permute-start(bf16[2,16,4096]{2,1,0:T(8,128)(2,1)S(1)} %get-tuple-element.33), channel_id=1, source_target_pairs={{0,4},{2,6},{4,0},{6,2},{8,12},{10,14},{12,8},{14,10},{1,5},{3,7},... | collective-permute-start | bytes 786440 | tf_op jit(solution)/shard_map/ppermute | solution.py:884
  15.2 11.6 %collective-permute-start.2 = (bf16[2,16,4096]{2,1,0:T(8,128)(2,1)S(1)}, bf16[2,16,4096]{2,1,0:T(8,128)(2,1)S(1)}, u32[]{:S(2)}, u32[]{:S(2)}) collective-permute-start(bf16[2,16,4096]{2,1,0:T(8,128)(2,1)S(1)} %get-tuple-element.34), channel_id=1, source_target_pairs={{0,6},{2,4},{4,2},{6,0},{8,14},{10,12},{12,10},{14,8},{1,7},{3,5},... | collective-permute-start | bytes 786440 | tf_op jit(solution)/shard_map/ppermute | solution.py:884
  27.8 14.5 %collective-permute-start.3 = (bf16[64,2048]{1,0:T(8,128)(2,1)S(1)}, bf16[64,2048]{1,0:T(8,128)(2,1)S(1)}, u32[]{:S(2)}, u32[]{:S(2)}) collective-permute-start(bf16[64,2048]{1,0:T(8,128)(2,1)S(1)} %get-tuple-element.36._), channel_id=1, source_target_pairs={{0,8},{2,10},{4,12},{6,14},{8,0},{10,2},{12,4},{14,6},{1,9},{3,11}... | collective-permute-start | bytes 786440 | tf_op jit(solution)/shard_map/ppermute | solution.py:903
  30.6 17.6 %collective-permute-start.5 = (bf16[2,16,4096]{2,1,0:T(8,128)(2,1)S(1)}, bf16[2,16,4096]{2,1,0:T(8,128)(2,1)S(1)}, u32[]{:S(2)}, u32[]{:S(2)}) collective-permute-start(bf16[2,16,4096]{2,1,0:T(8,128)(2,1)S(1)} %get-tuple-element.42), channel_id=1, source_target_pairs={{0,4},{2,6},{4,0},{6,2},{8,12},{10,14},{12,8},{14,10},{1,5},{3,7},... | collective-permute-start | bytes 786440 | tf_op jit(solution)/shard_map/ppermute | solution.py:884
  32.2 16.1 %collective-permute-start.6 = (bf16[2,16,4096]{2,1,0:T(8,128)(2,1)S(1)}, bf16[2,16,4096]{2,1,0:T(8,128)(2,1)S(1)}, u32[]{:S(2)}, u32[]{:S(2)}) collective-permute-start(bf16[2,16,4096]{2,1,0:T(8,128)(2,1)S(1)} %get-tuple-element.43), channel_id=1, source_target_pairs={{0,6},{2,4},{4,2},{6,0},{8,14},{10,12},{12,10},{14,8},{1,7},{3,5},... | collective-permute-start | bytes 786440 | tf_op jit(solution)/shard_map/ppermute | solution.py:884
  33.5 14.7 %collective-permute-start.4 = (bf16[2,16,4096]{2,1,0:T(8,128)(2,1)S(1)}, bf16[2,16,4096]{2,1,0:T(8,128)(2,1)S(1)}, u32[]{:S(2)}, u32[]{:S(2)}) collective-permute-start(bf16[2,16,4096]{2,1,0:T(8,128)(2,1)S(1)} %get-tuple-element.41), channel_id=1, source_target_pairs={{0,2},{2,0},{4,6},{6,4},{8,10},{10,8},{12,14},{14,12},{1,3},{3,1},... | collective-permute-start | bytes 786440 | tf_op jit(solution)/shard_map/ppermute | solution.py:884
  48.0 16.4 %collective-permute-start.10 = (bf16[64,2048]{1,0:T(8,128)(2,1)S(1)}, bf16[64,2048]{1,0:T(8,128)(2,1)S(1)}, u32[]{:S(2)}, u32[]{:S(2)}) collective-permute-start(bf16[64,2048]{1,0:T(8,128)(2,1)S(1)} %get-tuple-element.39.b_ref), channel_id=1, source_target_pairs={{0,8},{2,10},{4,12},{6,14},{8,0},{10,2},{12,4},{14,6},{1,9},{3,11}... | collective-permute-start | bytes 786440 | tf_op jit(solution)/shard_map/ppermute | solution.py:907
  50.3 12.2 %collective-permute-start.7 = (bf16[16,4096]{1,0:T(8,128)(2,1)S(1)}, bf16[16,4096]{1,0:T(8,128)(2,1)S(1)}, u32[]{:S(2)}, u32[]{:S(2)}) collective-permute-start(bf16[16,4096]{1,0:T(8,128)(2,1)S(1)} %get-tuple-element.47), channel_id=1, source_target_pairs={{0,2},{2,0},{4,6},{6,4},{8,10},{10,8},{12,14},{14,12},{1,3},{3,1},... | collective-permute-start | bytes 393224 | tf_op jit(solution)/shard_map/ppermute | solution.py:884
  52.0 10.6 %collective-permute-start.8 = (bf16[16,4096]{1,0:T(8,128)(2,1)S(1)}, bf16[16,4096]{1,0:T(8,128)(2,1)S(1)}, u32[]{:S(2)}, u32[]{:S(2)}) collective-permute-start(bf16[16,4096]{1,0:T(8,128)(2,1)S(1)} %get-tuple-element.48), channel_id=1, source_target_pairs={{0,4},{2,6},{4,0},{6,2},{8,12},{10,14},{12,8},{14,10},{1,5},{3,7},... | collective-permute-start | bytes 393224 | tf_op jit(solution)/shard_map/ppermute | solution.py:884
  54.9 9.4 %collective-permute-start.9 = (bf16[16,4096]{1,0:T(8,128)(2,1)S(1)}, bf16[16,4096]{1,0:T(8,128)(2,1)S(1)}, u32[]{:S(2)}, u32[]{:S(2)}) collective-permute-start(bf16[16,4096]{1,0:T(8,128)(2,1)S(1)} %get-tuple-element.49), channel_id=1, source_target_pairs={{0,6},{2,4},{4,2},{6,0},{8,14},{10,12},{12,10},{14,8},{1,7},{3,5},... | collective-permute-start | bytes 393224 | tf_op jit(solution)/shard_map/ppermute | solution.py:884
  65.4 28.6 %collective-permute-start.14 = (bf16[64,2048]{1,0:T(8,128)(2,1)S(1)}, bf16[64,2048]{1,0:T(8,128)(2,1)S(1)}, u32[]{:S(2)}, u32[]{:S(2)}) collective-permute-start(bf16[64,2048]{1,0:T(8,128)(2,1)S(1)} %get-tuple-element.58), channel_id=1, source_target_pairs={{0,8},{2,10},{4,12},{6,14},{8,0},{10,2},{12,4},{14,6},{1,9},{3,11}... | collective-permute-start | bytes 786440 | tf_op jit(solution)/shard_map/ppermute | solution.py:921
  67.0 9.2 %collective-permute-start.11 = (bf16[16,4096]{1,0:T(8,128)(2,1)S(1)}, bf16[16,4096]{1,0:T(8,128)(2,1)S(1)}, u32[]{:S(2)}, u32[]{:S(2)}) collective-permute-start(bf16[16,4096]{1,0:T(8,128)(2,1)S(1)} %get-tuple-element.54), channel_id=1, source_target_pairs={{0,2},{2,0},{4,6},{6,4},{8,10},{10,8},{12,14},{14,12},{1,3},{3,1},... | collective-permute-start | bytes 393224 | tf_op jit(solution)/shard_map/ppermute | solution.py:884
  67.6 12.5 %collective-permute-start.12 = (bf16[16,4096]{1,0:T(8,128)(2,1)S(1)}, bf16[16,4096]{1,0:T(8,128)(2,1)S(1)}, u32[]{:S(2)}, u32[]{:S(2)}) collective-permute-start(bf16[16,4096]{1,0:T(8,128)(2,1)S(1)} %get-tuple-element.55), channel_id=1, source_target_pairs={{0,4},{2,6},{4,0},{6,2},{8,12},{10,14},{12,8},{14,10},{1,5},{3,7},... | collective-permute-start | bytes 393224 | tf_op jit(solution)/shard_map/ppermute | solution.py:884
  71.0 10.4 %collective-permute-start.13 = (bf16[16,4096]{1,0:T(8,128)(2,1)S(1)}, bf16[16,4096]{1,0:T(8,128)(2,1)S(1)}, u32[]{:S(2)}, u32[]{:S(2)}) collective-permute-start(bf16[16,4096]{1,0:T(8,128)(2,1)S(1)} %get-tuple-element.56), channel_id=1, source_target_pairs={{0,6},{2,4},{4,2},{6,0},{8,14},{10,12},{12,10},{14,8},{1,7},{3,5},... | collective-permute-start | bytes 393224 | tf_op jit(solution)/shard_map/ppermute | solution.py:884
  71.0 24.9 %collective-permute-start.16 = (bf16[32,32,128]{2,1,0:T(8,128)(2,1)S(1)}, bf16[32,32,128]{2,1,0:T(8,128)(2,1)S(1)}, u32[]{:S(2)}, u32[]{:S(2)}) collective-permute-start(bf16[32,32,128]{2,1,0:T(8,128)(2,1)S(1)} %get-tuple-element.59.g0_ref), channel_id=1, source_target_pairs={{0,1},{1,0},{2,3},{3,2},{4,5},{5,4},{6,7},{7,6},{8,9},{9,8},{10,11... | collective-permute-start | bytes 786440 | tf_op jit(solution)/shard_map/ppermute | solution.py:924
  95.8 1.6 %collective-permute-start.15 = (bf16[32,32,128]{2,1,0:T(8,128)(2,1)S(1)}, bf16[32,32,128]{2,1,0:T(8,128)(2,1)S(1)}, u32[]{:S(2)}, u32[]{:S(2)}) collective-permute-start(bf16[32,32,128]{2,1,0:T(8,128)(2,1)S(1)} %volume_modes.1.u0_ref), channel_id=1, source_target_pairs={{0,1},{1,0},{2,3},{3,2},{4,5},{5,4},{6,7},{7,6},{8,9},{9,8},{10,11... | collective-permute-start | bytes 786440 | tf_op jit(solution)/shard_map/ppermute | solution.py:925

commit v3 on v1

--- a/solution.py
+++ b/solution.py
@@ -900,15 +900,16 @@
     vol_partner, _ = partner_modes(me, vol_received, ops, back_own, "volume_partner")
     vol_partner, *own_planes = back_planes(me, back_own, ops, vol_partner, "own_planes")
     back_near = in_square(own_planes)
+    early = nx * 3 // 8
     saved, back_near[0] = pointwise(
-        cot, kron, 0, nx // 2, own_planes[0], False, "pointwise_first"
+        cot, kron, 0, early, own_planes[0], False, "pointwise_first"
     )
     vol_partner, *other_planes = back_planes(
         me, back_other, ops, vol_partner, "partner_planes", back_near[1:], [saved]
     )
     back_far = in_square(other_planes)
     kept, back_far[0] = pointwise(
-        cot, kron, nx // 2, nx - nx // 2, other_planes[0], True, "pointwise_second"
+        cot, kron, early, nx - early, other_planes[0], True, "pointwise_second"
     )
     vol_other = lax.ppermute(vol_partner, "space", ACROSS)
     out = finish(me, back_near, back_far, saved, kept, ops)

time: 105 us -> 105 us (level)
  transfers between devices with their start and end apart: 17 -> 17, of which waited for: 5 -> 6; matrix products, arithmetic and copies ran while one was open for 0% -> 0% of each run, Pallas kernels for 50% -> 50%
where the time goes in v3:
time: 105 us; the launch traced here: 104 us
  Pallas kernels  70.9 us (68%)
  starting transfers between devices  21.4 us (20%)
  waiting for transfers between devices  10.2 us (10%)
  between operations  1.5 us (1%)
    pallas_call x2, Pallas kernels, lateral(): pl.pallas_call(lateral_kernel, in_specs=[SMEM, HBM, HBM, HBM, UNREAD], ou...  19.9 us
    ppermute x12, starting transfers between devices, in_square(): lax.ppermute(blocks[k], 'space', [(s, s ^ k) for s in range(8)])  16.6 us
    pallas_call x2, Pallas kernels, pointwise(): pl.pallas_call(functools.partial(pointwise_kernel if keep else pointwise_...  12.7 us
    pallas_call x1, Pallas kernels, finish(): pl.pallas_call(finish_kernel, in_specs=[SMEM] + [VMEM] * 8 + [HBM, VMEM,...  12.2 us
    ppermute x12, waiting for transfers between devices, in_square(): lax.ppermute(blocks[k], 'space', [(s, s ^ k) for s in range(8)])  8.7 us
    pallas_call x1, Pallas kernels, pack_weight(): pl.pallas_call(pack_kernel, in_specs=[SMEM, HBM, VMEM, HBM, UNREAD], out_...  7.53 us
    pallas_call x1, Pallas kernels, weight_grad(): pl.pallas_call(weight_grad_kernel, grid=(4,), in_specs=[SMEM] + [VMEM] *...  7.09 us
    pallas_call x1, Pallas kernels, back_modes(): pl.pallas_call(back_modes_kernel, in_specs=[SMEM] + [VMEM] * 5 + [HBM, VM...  5.67 us
  transfers between devices with their start and end apart: 17, of which 6 were waited for; matrix products, arithmetic and copies ran while one was open for 0% of the time, Pallas kernels for 50%

profile of v3, /device:TPU:0, one launch (start us, length us, event | category | flops | bytes accessed | tf_op | source)
XLA Modules:
  0.0 104.0 jit_solution(6198480166166445237)
XLA Ops:
  0.6 0.0 copy-start
  0.6 10.0 %cotangent_lateral.1 = (bf16[2,16,4096]{2,1,0:T(8,128)(2,1)S(1)}, bf16[2,16,4096]{2,1,0:T(8,128)(2,1)S(1)}, bf16[2,16,4096]{2,1,0:T(8,128)(2,1)S(1)}, bf16[2,16,4096]{2,1,0:T(8,128)(2,1)S(1)}) custom-call(s32[1]{0:T(128)} %bitcast.me_ref._, bf16[16,32,128,128]{3,2,1,0:T(8,128)(2,1)} %bitcast.8, bf16[1024,256]{1,0:T(8,128)(2,1)} %constant.18.clone.z_hbm, ...), custom_call_target="tpu_custom_call" | custom-call | flops 60000000 | bytes 1024 | tf_op jit(solution)/shard_map/cotangent_lateral/pallas_call | solution.py:277
  10.6 3.0 %collective-permute-start = (bf16[2,16,4096]{2,1,0:T(8,128)(2,1)S(1)}, bf16[2,16,4096]{2,1,0:T(8,128)(2,1)S(1)}, u32[]{:S(2)}, u32[]{:S(2)}) collective-permute-start(bf16[2,16,4096]{2,1,0:T(8,128)(2,1)S(1)} %get-tuple-element.32), channel_id=1, source_target_pairs={{0,2},{2,0},{4,6},{6,4},{8,10},{10,8},{12,14},{14,12},{1,3},{3,1},... | collective-permute-start | bytes 786440 | tf_op jit(solution)/shard_map/ppermute | solution.py:876
  13.6 1.6 %collective-permute-start.1 = (bf16[2,16,4096]{2,1,0:T(8,128)(2,1)S(1)}, bf16[2,16,4096]{2,1,0:T(8,128)(2,1)S(1)}, u32[]{:S(2)}, u32[]{:S(2)}) collective-permute-start(bf16[2,16,4096]{2,1,0:T(8,128)(2,1)S(1)} %get-tuple-element.33), channel_id=1, source_target_pairs={{0,4},{2,6},{4,0},{6,2},{8,12},{10,14},{12,8},{14,10},{1,5},{3,7},... | collective-permute-start | bytes 786440 | tf_op jit(solution)/shard_map/ppermute | solution.py:876
  15.2 0.0 collective-permute-start.2
  15.2 10.0 %volume_lateral.1 = (bf16[2,16,4096]{2,1,0:T(8,128)(2,1)S(1)}, bf16[2,16,4096]{2,1,0:T(8,128)(2,1)S(1)}, bf16[2,16,4096]{2,1,0:T(8,128)(2,1)S(1)}, bf16[2,16,4096]{2,1,0:T(8,128)(2,1)S(1)}) custom-call(s32[1]{0:T(128)} %bitcast.me_ref._, bf16[16,32,128,128]{3,2,1,0:T(8,128)(2,1)} %bitcast.12, bf16[1024,256]{1,0:T(8,128)(2,1)} %constant.18.clone.z_hbm, ...), custom_call_target="tpu_custom_call" | custom-call | flops 60000000 | bytes 1024 | tf_op jit(solution)/shard_map/volume_lateral/pallas_call | solution.py:277
  25.2 0.0 collective-permute-done.r1
  25.2 0.0 collective-permute-done.1.r2
  25.2 1.6 %collective-permute-done.2.r3 = bf16[2,16,4096]{2,1,0:T(8,128)(2,1)S(1)} collective-permute-done((bf16[2,16,4096]{2,1,0:T(8,128)(2,1)S(1)}, bf16[2,16,4096]{2,1,0:T(8,128)(2,1)S(1)}, u32[]{:S(2)}, u32[]{:S(2)}) %collective-permute-start.2) | collective-permute-done | bytes 262176 | tf_op jit(solution)/shard_map/ppermute | solution.py:876
  26.8 0.9 cotangent_partner.1
  27.8 2.8 %collective-permute-start.3 = (bf16[64,2048]{1,0:T(8,128)(2,1)S(1)}, bf16[64,2048]{1,0:T(8,128)(2,1)S(1)}, u32[]{:S(2)}, u32[]{:S(2)}) collective-permute-start(bf16[64,2048]{1,0:T(8,128)(2,1)S(1)} %get-tuple-element.36._), channel_id=1, source_target_pairs={{0,8},{2,10},{4,12},{6,14},{8,0},{10,2},{12,4},{14,6},{1,9},{3,11}... | collective-permute-start | bytes 786440 | tf_op jit(solution)/shard_map/ppermute | solution.py:895
  30.6 1.6 %collective-permute-start.5 = (bf16[2,16,4096]{2,1,0:T(8,128)(2,1)S(1)}, bf16[2,16,4096]{2,1,0:T(8,128)(2,1)S(1)}, u32[]{:S(2)}, u32[]{:S(2)}) collective-permute-start(bf16[2,16,4096]{2,1,0:T(8,128)(2,1)S(1)} %get-tuple-element.42), channel_id=1, source_target_pairs={{0,4},{2,6},{4,0},{6,2},{8,12},{10,14},{12,8},{14,10},{1,5},{3,7},... | collective-permute-start | bytes 786440 | tf_op jit(solution)/shard_map/ppermute | solution.py:876
  32.2 1.4 %collective-permute-start.6 = (bf16[2,16,4096]{2,1,0:T(8,128)(2,1)S(1)}, bf16[2,16,4096]{2,1,0:T(8,128)(2,1)S(1)}, u32[]{:S(2)}, u32[]{:S(2)}) collective-permute-start(bf16[2,16,4096]{2,1,0:T(8,128)(2,1)S(1)} %get-tuple-element.43), channel_id=1, source_target_pairs={{0,6},{2,4},{4,2},{6,0},{8,14},{10,12},{12,10},{14,8},{1,7},{3,5},... | collective-permute-start | bytes 786440 | tf_op jit(solution)/shard_map/ppermute | solution.py:876
  33.5 0.5 collective-permute-start.4
  34.7 0.0 copy-done
  34.7 7.5 %pack_weight.1 = (bf16[2,16,32,32,128]{4,3,2,1,0:T(8,128)(2,1)S(1)}, bf16[256,256]{1,0:T(8,128)(2,1)}) custom-call(s32[1]{0:T(128)S(6)} %copy.25.at_ref, bf16[2,32,32,32,64]{4,3,2,1,0:T(8,128)(2,1)} %bitcast.14, bf16[32,32]{1,0:T(8,128)(2,1)S(1)} %copy-done, bf16[32,4096]{1,0:T(8,128)(2,1)} %bitcast.15, bf16[64,2048]{1,0:T(8,128)(2,1)S(1)} %get-tuple-element.36._), custom_call_target="tpu_custom_call" | custom-call | flops 48000000 | bytes 1024 | tf_op jit(solution)/shard_map/pack_weight/pallas_call | solution.py:454
  42.3 0.0 collective-permute-done.3.other_ref
  42.3 5.7 %back_modes.1 = (bf16[32,32,128]{2,1,0:T(8,128)(2,1)S(1)}, bf16[64,2048]{1,0:T(8,128)(2,1)S(1)}) custom-call(s32[1]{0:T(128)} %bitcast.me_ref._, bf16[2,16,4096]{2,1,0:T(8,128)(2,1)S(1)} %get-tuple-element.31._.r0, bf16[2,16,4096]{2,1,0:T(8,128)(2,1)S(1)} %collective-permute-done.r1, bf16[2,16,4096]{2,1,0:T(8,128)(2,1)S(1)} %collective-permute-done.1.r2, ...), custom_call_target="tpu_custom_call" | custom-call | flops 36000000 | bytes 1024 | tf_op jit(solution)/shard_map/back_modes/pallas_call | solution.py:536
  48.0 0.2 collective-permute-start.10
  48.2 0.0 collective-permute-done.5.r2
  48.2 0.0 collective-permute-done.6.r3
  48.2 0.0 collective-permute-done.4.r1
  48.3 1.0 volume_partner.1
  49.2 1.1 %own_planes.1 = (bf16[64,2048]{1,0:T(8,128)(2,1)S(1)}, bf16[16,4096]{1,0:T(8,128)(2,1)S(1)}, bf16[16,4096]{1,0:T(8,128)(2,1)S(1)}, bf16[16,4096]{1,0:T(8,128)(2,1)S(1)}, bf16[16,4096]{1,0:T(8,128)(2,1)S(1)}) custom-call(s32[1]{0:T(128)} %bitcast.me_ref._, bf16[64,2048]{1,0:T(8,128)(2,1)S(1)} %get-tuple-element.39.b_ref, ...), custom_call_target="tpu_custom_call", output_to_operand_aliasing={{0}: (3, {})} | custom-call | flops 6000000 | bytes 1024 | tf_op jit(solution)/shard_map/own_planes/pallas_call | solution.py:574
  50.3 1.7 %collective-permute-start.7 = (bf16[16,4096]{1,0:T(8,128)(2,1)S(1)}, bf16[16,4096]{1,0:T(8,128)(2,1)S(1)}, u32[]{:S(2)}, u32[]{:S(2)}) collective-permute-start(bf16[16,4096]{1,0:T(8,128)(2,1)S(1)} %get-tuple-element.47), channel_id=1, source_target_pairs={{0,2},{2,0},{4,6},{6,4},{8,10},{10,8},{12,14},{14,12},{1,3},{3,1},... | collective-permute-start | bytes 393224 | tf_op jit(solution)/shard_map/ppermute | solution.py:876
  52.0 2.9 %collective-permute-start.8 = (bf16[16,4096]{1,0:T(8,128)(2,1)S(1)}, bf16[16,4096]{1,0:T(8,128)(2,1)S(1)}, u32[]{:S(2)}, u32[]{:S(2)}) collective-permute-start(bf16[16,4096]{1,0:T(8,128)(2,1)S(1)} %get-tuple-element.48), channel_id=1, source_target_pairs={{0,4},{2,6},{4,0},{6,2},{8,12},{10,14},{12,8},{14,10},{1,5},{3,7},... | collective-permute-start | bytes 393224 | tf_op jit(solution)/shard_map/ppermute | solution.py:876
  54.9 0.0 collective-permute-start.9
  54.9 6.6 %pointwise_first.1 = (bf16[6,32,128,128]{3,2,1,0:T(8,128)(2,1)}, bf16[16,4096]{1,0:T(8,128)(2,1)S(1)}) custom-call(bf16[16,32,128,128]{3,2,1,0:T(8,128)(2,1)} %bitcast.9, bf16[256,256]{1,0:T(8,128)(2,1)} %get-tuple-element.37.k_hbm, bf16[16,4096]{1,0:T(8,128)(2,1)S(1)} %get-tuple-element.45._), custom_call_target="tpu_custom_call", output_to_operand_aliasing={{1}: (2, {})} | custom-call | flops 30000000 | bytes 1024 | tf_op jit(solution)/shard_map/pointwise_first/pallas_call | solution.py:737
  61.5 0.0 collective-permute-done.7.rest_1_.n1
  61.5 1.1 %collective-permute-done.8.rest_2_.n2 = bf16[16,4096]{1,0:T(8,128)(2,1)S(1)} collective-permute-done((bf16[16,4096]{1,0:T(8,128)(2,1)S(1)}, bf16[16,4096]{1,0:T(8,128)(2,1)S(1)}, u32[]{:S(2)}, u32[]{:S(2)}) %collective-permute-start.8) | collective-permute-done | bytes 131104 | tf_op jit(solution)/shard_map/ppermute | solution.py:876
  62.6 1.8 %collective-permute-done.9.rest_3_.n3 = bf16[16,4096]{1,0:T(8,128)(2,1)S(1)} collective-permute-done((bf16[16,4096]{1,0:T(8,128)(2,1)S(1)}, bf16[16,4096]{1,0:T(8,128)(2,1)S(1)}, u32[]{:S(2)}, u32[]{:S(2)}) %collective-permute-start.9) | collective-permute-done | bytes 131104 | tf_op jit(solution)/shard_map/ppermute | solution.py:876
  64.3 0.0 collective-permute-done.10.b_ref
  64.4 1.1 %partner_planes.1 = (bf16[64,2048]{1,0:T(8,128)(2,1)S(1)}, bf16[16,4096]{1,0:T(8,128)(2,1)S(1)}, bf16[16,4096]{1,0:T(8,128)(2,1)S(1)}, bf16[16,4096]{1,0:T(8,128)(2,1)S(1)}, bf16[16,4096]{1,0:T(8,128)(2,1)S(1)}) custom-call(s32[1]{0:T(128)} %bitcast.me_ref._, bf16[64,2048]{1,0:T(8,128)(2,1)S(1)} %collective-permute-done.10.b_ref, ...), custom_call_target="tpu_custom_call", output_to_operand_aliasing={{0}: (3, {})} | custom-call | flops 6000000 | bytes 1024 | tf_op jit(solution)/shard_map/partner_planes/pallas_call | solution.py:574
  65.4 1.6 %collective-permute-start.14 = (bf16[64,2048]{1,0:T(8,128)(2,1)S(1)}, bf16[64,2048]{1,0:T(8,128)(2,1)S(1)}, u32[]{:S(2)}, u32[]{:S(2)}) collective-permute-start(bf16[64,2048]{1,0:T(8,128)(2,1)S(1)} %get-tuple-element.58), channel_id=1, source_target_pairs={{0,8},{2,10},{4,12},{6,14},{8,0},{10,2},{12,4},{14,6},{1,9},{3,11}... | collective-permute-start | bytes 786440 | tf_op jit(solution)/shard_map/ppermute | solution.py:914
  67.0 0.5 collective-permute-start.11
  67.6 3.4 %collective-permute-start.12 = (bf16[16,4096]{1,0:T(8,128)(2,1)S(1)}, bf16[16,4096]{1,0:T(8,128)(2,1)S(1)}, u32[]{:S(2)}, u32[]{:S(2)}) collective-permute-start(bf16[16,4096]{1,0:T(8,128)(2,1)S(1)} %get-tuple-element.55), channel_id=1, source_target_pairs={{0,4},{2,6},{4,0},{6,2},{8,12},{10,14},{12,8},{14,10},{1,5},{3,7},... | collective-permute-start | bytes 393224 | tf_op jit(solution)/shard_map/ppermute | solution.py:876
  71.0 0.0 collective-permute-start.13
  71.0 0.0 collective-permute-start.16
  71.0 6.1 %pointwise_second.1 = (bf16[10,32,128,128]{3,2,1,0:T(8,128)(2,1)S(1)}, bf16[16,4096]{1,0:T(8,128)(2,1)S(1)}) custom-call(bf16[16,32,128,128]{3,2,1,0:T(8,128)(2,1)} %bitcast.10, bf16[256,256]{1,0:T(8,128)(2,1)} %get-tuple-element.37.k_hbm, bf16[16,4096]{1,0:T(8,128)(2,1)S(1)} %get-tuple-element.52._), custom_call_target="tpu_custom_call", output_to_operand_aliasing={{1}: (2, {})} | custom-call | flops 30000000 | bytes 1024 | tf_op jit(solution)/shard_map/pointwise_second/pallas_call | solution.py:737
  77.1 0.0 collective-permute-done.11.f1
  77.1 3.0 %collective-permute-done.12.f2 = bf16[16,4096]{1,0:T(8,128)(2,1)S(1)} collective-permute-done((bf16[16,4096]{1,0:T(8,128)(2,1)S(1)}, bf16[16,4096]{1,0:T(8,128)(2,1)S(1)}, u32[]{:S(2)}, u32[]{:S(2)}) %collective-permute-start.12) | collective-permute-done | bytes 131104 | tf_op jit(solution)/shard_map/ppermute | solution.py:876
  80.1 1.3 %collective-permute-done.13.f3 = bf16[16,4096]{1,0:T(8,128)(2,1)S(1)} collective-permute-done((bf16[16,4096]{1,0:T(8,128)(2,1)S(1)}, bf16[16,4096]{1,0:T(8,128)(2,1)S(1)}, u32[]{:S(2)}, u32[]{:S(2)}) %collective-permute-start.13) | collective-permute-done | bytes 131104 | tf_op jit(solution)/shard_map/ppermute | solution.py:876
  81.4 12.2 %finish.1.rest_0_ = bf16[16,32,128,128]{3,2,1,0:T(8,128)(2,1)} custom-call(s32[1]{0:T(128)} %bitcast.me_ref._, bf16[16,4096]{1,0:T(8,128)(2,1)S(1)} %get-tuple-element.46.n0, bf16[16,4096]{1,0:T(8,128)(2,1)S(1)} %collective-permute-done.7.rest_1_.n1, bf16[16,4096]{1,0:T(8,128)(2,1)S(1)} %collective-permute-done.8.rest_2_.n2, ...), custom_call_target="tpu_custom_call" | custom-call | flops 72000000 | bytes 1024 | tf_op jit(solution)/shard_map/finish/pallas_call | solution.py:846
  93.6 0.0 collective-permute-done.14.other_ref
  93.6 1.7 %volume_modes.1.u0_ref = bf16[32,32,128]{2,1,0:T(8,128)(2,1)S(1)} custom-call(s32[1]{0:T(128)} %bitcast.me_ref._, bf16[2,16,4096]{2,1,0:T(8,128)(2,1)S(1)} %get-tuple-element.40.r0, bf16[2,16,4096]{2,1,0:T(8,128)(2,1)S(1)} %collective-permute-done.4.r1, bf16[2,16,4096]{2,1,0:T(8,128)(2,1)S(1)} %collective-permute-done.5.r2, ...), custom_call_target="tpu_custom_call" | custom-call | flops 9000000 | bytes 1024 | tf_op jit(solution)/shard_map/volume_modes/pallas_call | solution.py:386
  95.4 0.1 collective-permute-start.15
  95.4 0.0 collective-permute-done.16.g1_ref
  95.4 1.5 %collective-permute-done.15.u1_ref = bf16[32,32,128]{2,1,0:T(8,128)(2,1)S(1)} collective-permute-done((bf16[32,32,128]{2,1,0:T(8,128)(2,1)S(1)}, bf16[32,32,128]{2,1,0:T(8,128)(2,1)S(1)}, u32[]{:S(2)}, u32[]{:S(2)}) %collective-permute-start.15) | collective-permute-done | bytes 262176 | tf_op jit(solution)/shard_map/ppermute | solution.py:918
  97.0 7.1 %weight_grad.1 = f32[2,32,32,16,64]{4,3,2,1,0:T(8,128)} custom-call(s32[1]{0:T(128)} %bitcast.6.half_ref, bf16[32,32,128]{2,1,0:T(8,128)(2,1)S(1)} %volume_modes.1.u0_ref, bf16[32,32,128]{2,1,0:T(8,128)(2,1)S(1)} %collective-permute-done.15.u1_ref, bf16[32,32,128]{2,1,0:T(8,128)(2,1)S(1)} %get-tuple-element.59.g0_ref, ...), custom_call_target="tpu_custom_call" | custom-call | flops 48000000 | bytes 1024 | tf_op jit(solution)/shard_map/weight_grad/pallas_call | solution.py:624
  (1 shorter events, 0.0 us)
Async XLA Ops:
  0.6 34.1 %copy-start = (bf16[32,32]{1,0:T(8,128)(2,1)S(1)}, bf16[32,32]{1,0:T(8,128)(2,1)}, u32[]{:S(2)}) copy-start(bf16[32,32]{1,0:T(8,128)(2,1)} %p_ref.1) | copy-start | bytes 6148
  10.6 14.6 %collective-permute-start = (bf16[2,16,4096]{2,1,0:T(8,128)(2,1)S(1)}, bf16[2,16,4096]{2,1,0:T(8,128)(2,1)S(1)}, u32[]{:S(2)}, u32[]{:S(2)}) collective-permute-start(bf16[2,16,4096]{2,1,0:T(8,128)(2,1)S(1)} %get-tuple-element.32), channel_id=1, source_target_pairs={{0,2},{2,0},{4,6},{6,4},{8,10},{10,8},{12,14},{14,12},{1,3},{3,1},... | collective-permute-start | bytes 786440 | tf_op jit(solution)/shard_map/ppermute | solution.py:876
  13.6 11.6 %collective-permute-start.1 = (bf16[2,16,4096]{2,1,0:T(8,128)(2,1)S(1)}, bf16[2,16,4096]{2,1,0:T(8,128)(2,1)S(1)}, u32[]{:S(2)}, u32[]{:S(2)}) collective-permute-start(bf16[2,16,4096]{2,1,0:T(8,128)(2,1)S(1)} %get-tuple-element.33), channel_id=1, source_target_pairs={{0,4},{2,6},{4,0},{6,2},{8,12},{10,14},{12,8},{14,10},{1,5},{3,7},... | collective-permute-start | bytes 786440 | tf_op jit(solution)/shard_map/ppermute | solution.py:876
  15.2 11.6 %collective-permute-start.2 = (bf16[2,16,4096]{2,1,0:T(8,128)(2,1)S(1)}, bf16[2,16,4096]{2,1,0:T(8,128)(2,1)S(1)}, u32[]{:S(2)}, u32[]{:S(2)}) collective-permute-start(bf16[2,16,4096]{2,1,0:T(8,128)(2,1)S(1)} %get-tuple-element.34), channel_id=1, source_target_pairs={{0,6},{2,4},{4,2},{6,0},{8,14},{10,12},{12,10},{14,8},{1,7},{3,5},... | collective-permute-start | bytes 786440 | tf_op jit(solution)/shard_map/ppermute | solution.py:876
  27.8 14.5 %collective-permute-start.3 = (bf16[64,2048]{1,0:T(8,128)(2,1)S(1)}, bf16[64,2048]{1,0:T(8,128)(2,1)S(1)}, u32[]{:S(2)}, u32[]{:S(2)}) collective-permute-start(bf16[64,2048]{1,0:T(8,128)(2,1)S(1)} %get-tuple-element.36._), channel_id=1, source_target_pairs={{0,8},{2,10},{4,12},{6,14},{8,0},{10,2},{12,4},{14,6},{1,9},{3,11}... | collective-permute-start | bytes 786440 | tf_op jit(solution)/shard_map/ppermute | solution.py:895
  30.6 17.6 %collective-permute-start.5 = (bf16[2,16,4096]{2,1,0:T(8,128)(2,1)S(1)}, bf16[2,16,4096]{2,1,0:T(8,128)(2,1)S(1)}, u32[]{:S(2)}, u32[]{:S(2)}) collective-permute-start(bf16[2,16,4096]{2,1,0:T(8,128)(2,1)S(1)} %get-tuple-element.42), channel_id=1, source_target_pairs={{0,4},{2,6},{4,0},{6,2},{8,12},{10,14},{12,8},{14,10},{1,5},{3,7},... | collective-permute-start | bytes 786440 | tf_op jit(solution)/shard_map/ppermute | solution.py:876
  32.2 16.1 %collective-permute-start.6 = (bf16[2,16,4096]{2,1,0:T(8,128)(2,1)S(1)}, bf16[2,16,4096]{2,1,0:T(8,128)(2,1)S(1)}, u32[]{:S(2)}, u32[]{:S(2)}) collective-permute-start(bf16[2,16,4096]{2,1,0:T(8,128)(2,1)S(1)} %get-tuple-element.43), channel_id=1, source_target_pairs={{0,6},{2,4},{4,2},{6,0},{8,14},{10,12},{12,10},{14,8},{1,7},{3,5},... | collective-permute-start | bytes 786440 | tf_op jit(solution)/shard_map/ppermute | solution.py:876
  33.5 14.7 %collective-permute-start.4 = (bf16[2,16,4096]{2,1,0:T(8,128)(2,1)S(1)}, bf16[2,16,4096]{2,1,0:T(8,128)(2,1)S(1)}, u32[]{:S(2)}, u32[]{:S(2)}) collective-permute-start(bf16[2,16,4096]{2,1,0:T(8,128)(2,1)S(1)} %get-tuple-element.41), channel_id=1, source_target_pairs={{0,2},{2,0},{4,6},{6,4},{8,10},{10,8},{12,14},{14,12},{1,3},{3,1},... | collective-permute-start | bytes 786440 | tf_op jit(solution)/shard_map/ppermute | solution.py:876
  48.0 16.4 %collective-permute-start.10 = (bf16[64,2048]{1,0:T(8,128)(2,1)S(1)}, bf16[64,2048]{1,0:T(8,128)(2,1)S(1)}, u32[]{:S(2)}, u32[]{:S(2)}) collective-permute-start(bf16[64,2048]{1,0:T(8,128)(2,1)S(1)} %get-tuple-element.39.b_ref), channel_id=1, source_target_pairs={{0,8},{2,10},{4,12},{6,14},{8,0},{10,2},{12,4},{14,6},{1,9},{3,11}... | collective-permute-start | bytes 786440 | tf_op jit(solution)/shard_map/ppermute | solution.py:899
  50.3 11.2 %collective-permute-start.7 = (bf16[16,4096]{1,0:T(8,128)(2,1)S(1)}, bf16[16,4096]{1,0:T(8,128)(2,1)S(1)}, u32[]{:S(2)}, u32[]{:S(2)}) collective-permute-start(bf16[16,4096]{1,0:T(8,128)(2,1)S(1)} %get-tuple-element.47), channel_id=1, source_target_pairs={{0,2},{2,0},{4,6},{6,4},{8,10},{10,8},{12,14},{14,12},{1,3},{3,1},... | collective-permute-start | bytes 393224 | tf_op jit(solution)/shard_map/ppermute | solution.py:876
  52.0 10.6 %collective-permute-start.8 = (bf16[16,4096]{1,0:T(8,128)(2,1)S(1)}, bf16[16,4096]{1,0:T(8,128)(2,1)S(1)}, u32[]{:S(2)}, u32[]{:S(2)}) collective-permute-start(bf16[16,4096]{1,0:T(8,128)(2,1)S(1)} %get-tuple-element.48), channel_id=1, source_target_pairs={{0,4},{2,6},{4,0},{6,2},{8,12},{10,14},{12,8},{14,10},{1,5},{3,7},... | collective-permute-start | bytes 393224 | tf_op jit(solution)/shard_map/ppermute | solution.py:876
  54.9 9.4 %collective-permute-start.9 = (bf16[16,4096]{1,0:T(8,128)(2,1)S(1)}, bf16[16,4096]{1,0:T(8,128)(2,1)S(1)}, u32[]{:S(2)}, u32[]{:S(2)}) collective-permute-start(bf16[16,4096]{1,0:T(8,128)(2,1)S(1)} %get-tuple-element.49), channel_id=1, source_target_pairs={{0,6},{2,4},{4,2},{6,0},{8,14},{10,12},{12,10},{14,8},{1,7},{3,5},... | collective-permute-start | bytes 393224 | tf_op jit(solution)/shard_map/ppermute | solution.py:876
  65.4 28.2 %collective-permute-start.14 = (bf16[64,2048]{1,0:T(8,128)(2,1)S(1)}, bf16[64,2048]{1,0:T(8,128)(2,1)S(1)}, u32[]{:S(2)}, u32[]{:S(2)}) collective-permute-start(bf16[64,2048]{1,0:T(8,128)(2,1)S(1)} %get-tuple-element.58), channel_id=1, source_target_pairs={{0,8},{2,10},{4,12},{6,14},{8,0},{10,2},{12,4},{14,6},{1,9},{3,11}... | collective-permute-start | bytes 786440 | tf_op jit(solution)/shard_map/ppermute | solution.py:914
  67.0 10.1 %collective-permute-start.11 = (bf16[16,4096]{1,0:T(8,128)(2,1)S(1)}, bf16[16,4096]{1,0:T(8,128)(2,1)S(1)}, u32[]{:S(2)}, u32[]{:S(2)}) collective-permute-start(bf16[16,4096]{1,0:T(8,128)(2,1)S(1)} %get-tuple-element.54), channel_id=1, source_target_pairs={{0,2},{2,0},{4,6},{6,4},{8,10},{10,8},{12,14},{14,12},{1,3},{3,1},... | collective-permute-start | bytes 393224 | tf_op jit(solution)/shard_map/ppermute | solution.py:876
  67.6 12.5 %collective-permute-start.12 = (bf16[16,4096]{1,0:T(8,128)(2,1)S(1)}, bf16[16,4096]{1,0:T(8,128)(2,1)S(1)}, u32[]{:S(2)}, u32[]{:S(2)}) collective-permute-start(bf16[16,4096]{1,0:T(8,128)(2,1)S(1)} %get-tuple-element.55), channel_id=1, source_target_pairs={{0,4},{2,6},{4,0},{6,2},{8,12},{10,14},{12,8},{14,10},{1,5},{3,7},... | collective-permute-start | bytes 393224 | tf_op jit(solution)/shard_map/ppermute | solution.py:876
  71.0 10.4 %collective-permute-start.13 = (bf16[16,4096]{1,0:T(8,128)(2,1)S(1)}, bf16[16,4096]{1,0:T(8,128)(2,1)S(1)}, u32[]{:S(2)}, u32[]{:S(2)}) collective-permute-start(bf16[16,4096]{1,0:T(8,128)(2,1)S(1)} %get-tuple-element.56), channel_id=1, source_target_pairs={{0,6},{2,4},{4,2},{6,0},{8,14},{10,12},{12,10},{14,8},{1,7},{3,5},... | collective-permute-start | bytes 393224 | tf_op jit(solution)/shard_map/ppermute | solution.py:876
  71.0 24.5 %collective-permute-start.16 = (bf16[32,32,128]{2,1,0:T(8,128)(2,1)S(1)}, bf16[32,32,128]{2,1,0:T(8,128)(2,1)S(1)}, u32[]{:S(2)}, u32[]{:S(2)}) collective-permute-start(bf16[32,32,128]{2,1,0:T(8,128)(2,1)S(1)} %get-tuple-element.59.g0_ref), channel_id=1, source_target_pairs={{0,1},{1,0},{2,3},{3,2},{4,5},{5,4},{6,7},{7,6},{8,9},{9,8},{10,11... | collective-permute-start | bytes 786440 | tf_op jit(solution)/shard_map/ppermute | solution.py:917
  95.4 1.6 %collective-permute-start.15 = (bf16[32,32,128]{2,1,0:T(8,128)(2,1)S(1)}, bf16[32,32,128]{2,1,0:T(8,128)(2,1)S(1)}, u32[]{:S(2)}, u32[]{:S(2)}) collective-permute-start(bf16[32,32,128]{2,1,0:T(8,128)(2,1)S(1)} %volume_modes.1.u0_ref), channel_id=1, source_target_pairs={{0,1},{1,0},{2,3},{3,2},{4,5},{5,4},{6,7},{7,6},{8,9},{9,8},{10,11... | collective-permute-start | bytes 786440 | tf_op jit(solution)/shard_map/ppermute | solution.py:918
